TPU v7x, 256 devices: a whole 4x4x8 slice. The times are simulated.
256 devices in a mesh: tm: 64 (over y, z_hi, x, core), elem: 4 (over z_lo).
Axes of the slice: x: 4, y: 4, z: 8 (z_hi: 2, z_lo: 4; z = z_hi * 4 + z_lo), core: 2. Of those that a mesh axis runs over, the one named last changes fastest.
Arguments:
- samples: float32 [2, 512, 196608], P(None, 'elem', 'tm'), may hold values from -24 to 24
- shift_bin: int32 [1], replicated, may hold values from 1 to 63
- start_vectors: int32 [2, 512, 64], P(None, 'elem'), may hold values from 0 to 8
- tap_table: int32 [4, 1024], replicated, may hold values from -2048 to 2047
Outputs:
- spectra: float32 [2, 64, 192, 1024], P(None, 'elem', 'tm')
- weights: float32 [2, 512, 64], P(None, 'elem')
All inputs are finite; a program needn't handle non-finite values.
Results may differ from a plain program's by a relative error of at most 0.0003.
Values sent between devices are 32-bit elements; how exact they have to be, the bound alone decides.
A program may use at most 128 MiB of HBM per device.

v0:
```python
import math

import jax
import jax.numpy as jnp
from jax import lax
from jax.sharding import PartitionSpec as P

ELEMS = 512
BEAMS = 64
CHANNELS = 1024
TAPS = 4
ITERS = 3


EPS = 1e-06
HIGH = lax.Precision.HIGHEST


def from_behind(x, axis, by):
    devices = lax.axis_size(axis)
    pairs = [(i, i + by) for i in range(devices) if 0 <= i + by < devices]
    return lax.ppermute(x, axis, pairs)


def rotation(shift_bin, offset, count, modulus):
    times = offset + lax.iota(jnp.int32, count)
    folded = shift_bin[0] * times % modulus
    angle = 2.0 * math.pi / modulus * folded.astype(jnp.float32)
    return (jnp.cos(angle), jnp.sin(angle))


def stacked_left(sig_real, sig_imag, cos_table, sin_table):
    mod_real = sig_real * cos_table + sig_imag * sin_table
    mod_imag = sig_imag * cos_table - sig_real * sin_table
    return jnp.concatenate([sig_real, sig_imag, mod_real, mod_imag], 0)


def contract(left_rows, right_rows):
    return lax.dot_general(
        left_rows,
        right_rows,
        (((1,), (1,)), ((), ())),
        precision=HIGH,
        preferred_element_type=jnp.float32,
    )


def transposed(left_rows, right_rows):
    return lax.dot_general(
        left_rows,
        right_rows,
        (((0,), (0,)), ((), ())),
        precision=HIGH,
        preferred_element_type=jnp.float32,
    )


def matmul(left_rows, right_rows):
    return jnp.dot(left_rows, right_rows, precision=HIGH, preferred_element_type=jnp.float32)


def correlate(left_rows, right_pair, row_count):
    right_rows = jnp.concatenate([right_pair[0], right_pair[1]], 0)
    grams = contract(left_rows, right_rows)
    col_count = right_pair.shape[1]

    def block(row_block, col_block):
        return grams[
            row_block * row_count : (row_block + 1) * row_count,
            col_block * col_count : (col_block + 1) * col_count,
        ]

    return jnp.stack(
        [
            block(0, 0) + block(1, 1),
            block(1, 0) - block(0, 1),
            block(2, 0) + block(3, 1),
            block(3, 0) - block(2, 1),
        ]
    )


def column_squares(vector):
    return jnp.sum(vector * vector, axis=(0, 1))


def column_norms(vector):
    return lax.psum(column_squares(vector), "elem")


def body(samples, shift_bin, start_vectors, tap_table):
    span_len = samples.shape[2]
    elem_count = lax.axis_size("elem")
    modulus = span_len * lax.axis_size("tm")
    elems_dev = samples.shape[1]
    span_start = lax.axis_index("tm") * span_len
    cos_table, sin_table = rotation(shift_bin, span_start, span_len, modulus)
    left_rows = stacked_left(samples[0], samples[1], cos_table, sin_table)
    partial_corr = correlate(
        left_rows, lax.all_gather(samples, "elem", axis=1, tiled=True), elems_dev
    )
    summed_corr = lax.psum(partial_corr, "tm")
    plain_real = summed_corr[0] / modulus
    plain_imag = summed_corr[1] / modulus
    cyc_scale = 1.0 / math.sqrt(modulus * ELEMS)
    cyc_real = summed_corr[2] * cyc_scale
    cyc_imag = summed_corr[3] * cyc_scale
    row_start = lax.axis_index("elem") * elems_dev
    initial = start_vectors.astype(jnp.float32) - 4.5
    vector = initial / jnp.sqrt(column_norms(initial) + EPS)
    for iteration in range(ITERS):
        adjoint_vec_real = vector[0]
        adjoint_vec_imag = vector[1]
        adj_real = transposed(cyc_real, adjoint_vec_real) + transposed(cyc_imag, adjoint_vec_imag)
        adj_imag = transposed(cyc_real, adjoint_vec_imag) - transposed(cyc_imag, adjoint_vec_real)
        herm_real = transposed(plain_real, adjoint_vec_real) + transposed(
            plain_imag, adjoint_vec_imag
        )
        herm_imag = transposed(plain_real, adjoint_vec_imag) - transposed(
            plain_imag, adjoint_vec_real
        )
        summed = lax.psum(jnp.stack([adj_real, adj_imag, herm_real, herm_imag]), "elem")
        own_plain = lax.dynamic_slice_in_dim(summed[2:4], row_start, elems_dev, 1)
        out_real = matmul(cyc_real, summed[0]) - matmul(cyc_imag, summed[1]) + own_plain[0]
        out_imag = matmul(cyc_real, summed[1]) + matmul(cyc_imag, summed[0]) + own_plain[1]
        vector = jnp.stack([out_real, out_imag])
        vector = vector / jnp.sqrt(column_norms(vector) + EPS)
    vec_real, vec_imag = (vector[0], vector[1])
    beam_real = transposed(vec_real, samples[0]) + transposed(vec_imag, samples[1])
    beam_imag = transposed(vec_real, samples[1]) - transposed(vec_imag, samples[0])
    beam_partial = jnp.stack([beam_real, beam_imag])
    beams_dev = BEAMS // elem_count
    beam_all = lax.psum(beam_partial, "elem")
    own_beams = lax.dynamic_slice_in_dim(beam_all, lax.axis_index("elem") * beams_dev, beams_dev, 1)
    earlier = from_behind(own_beams, "tm", 1)
    frames = span_len // CHANNELS
    extended = jnp.concatenate([earlier, own_beams], 2).reshape(
        2, beams_dev, TAPS - 1 + frames, CHANNELS
    )
    taps = tap_table.astype(jnp.float32) / 2048.0
    folded = jnp.zeros((2, beams_dev, frames, CHANNELS), jnp.float32)
    for tap in range(TAPS):
        folded = folded + taps[tap] * extended[:, :, TAPS - 1 - tap : TAPS - 1 - tap + frames, :]
    channel_ids = lax.iota(jnp.int32, CHANNELS)
    products = channel_ids[:, None] * channel_ids[None, :] % CHANNELS
    angle = 2.0 * math.pi / CHANNELS * products.astype(jnp.float32)
    cos_dft = jnp.cos(angle)
    sin_dft = jnp.sin(angle)
    fold_real = folded[0].reshape(beams_dev * frames, CHANNELS)
    fold_imag = folded[1].reshape(beams_dev * frames, CHANNELS)
    norm_factor = 1.0 / math.sqrt(CHANNELS)
    spec_real = (matmul(fold_real, cos_dft) + matmul(fold_imag, sin_dft)) * norm_factor
    spec_imag = (matmul(fold_imag, cos_dft) - matmul(fold_real, sin_dft)) * norm_factor
    spectra = jnp.stack([spec_real, spec_imag]).reshape(2, beams_dev, frames, CHANNELS)
    return (spectra, vector)


def solution(mesh):
    return jax.shard_map(
        body,
        mesh=mesh,
        in_specs=(P(None, "elem", "tm"), P(), P(None, "elem", None), P()),
        out_specs=(P(None, "elem", "tm", None), P(None, "elem", None)),
        check_vma=False,
    )
```

profile of v0, /device:TPU:40, one launch (start us, length us, event | category | flops | bytes accessed | tf_op | source)
XLA Modules:
  0.0 1463.4 jit_solution(7564740597796092401)
XLA Ops:
  9.1 1.9 slice_bitcast_fusion.3
  10.9 2.1 multiply_add_fusion
  13.0 220.8 %all-gather.2.cloned.1.call-done = f32[2,512,3072]{2,1,0:T(8,128)} async-done(((f32[2,128,3072]{2,1,0:T(8,128)}), f32[2,512,3072]{2,1,0:T(8,128)}) %all-gather.2.cloned.1.call-update) | async-done | bytes 12582928 | tf_op jit(solution)/shard_map/all_gather | solution.py:100
  233.8 8.4 slice_bitcast_fusion.1
  242.2 23.2 %fusion = f32[512,1024]{1,0:T(8,128)S(1)} fusion(f32[512,3072]{1,0:T(8,128)} %get-tuple-element.5, f32[512,3072]{1,0:T(8,128)S(1)} %get-tuple-element.4, f32[128,3072]{1,0:T(8,128)} %get-tuple-element.7, f32[128,3072]{1,0:T(8,128)} %get-tuple-element.6, f32[128,3072]{1,0:T(8,128)} %get-tuple-element.9, f32[128,3072]{1,0:T(8,128)} %get-tuple-element.8), kind=kOutput, calls=%fused_computation | convolution fusion | flops 19335217152 | bytes 20971520 | tf_op jit(solution)/shard_map/dot_general | solution.py:39
  267.0 9.7 psum.64
  276.8 738.7 %all-reduce.6.cloned.1.call-done = f32[4,128,512]{2,1,0:T(8,128)} async-done(((f32[4,128,512]{2,1,0:T(8,128)}), f32[4,128,512]{2,1,0:T(8,128)}) %all-reduce.6.cloned.1.call-update) | async-done | bytes 1048592 | tf_op jit(solution)/shard_map/psum | solution.py:102
  1015.5 1.3 fusion.90
  1026.6 84.4 %all-reduce.8.cloned.1.call-done = f32[4,512,64]{1,2,0:T(8,128)} async-done(((f32[4,512,64]{1,2,0:T(8,128)}), f32[4,512,64]{1,2,0:T(8,128)}) %all-reduce.8.cloned.1.call-update) | async-done | bytes 524304 | tf_op jit(solution)/shard_map/psum | solution.py:122
  1111.0 1.3 fusion.77
  1113.2 1.3 fusion.76
  1114.5 1.3 fusion.64
  1115.9 1.3 fusion.62
  1117.3 11.6 psum.66
  1132.4 51.3 %all-reduce.10.cloned.1.call-done = f32[4,512,64]{1,2,0:T(8,128)} async-done(((f32[4,512,64]{1,2,0:T(8,128)}), f32[4,512,64]{1,2,0:T(8,128)}) %all-reduce.10.cloned.1.call-update) | async-done | bytes 524304 | tf_op jit(solution)/shard_map/psum | solution.py:122
  1186.0 1.3 fusion.78
  1187.3 1.3 fusion.58
  1188.6 1.3 fusion.60
  1190.0 11.1 psum.68
  1204.7 51.2 %all-reduce.12.cloned.1.call-done = f32[4,512,64]{1,2,0:T(8,128)} async-done(((f32[4,512,64]{1,2,0:T(8,128)}), f32[4,512,64]{1,2,0:T(8,128)}) %all-reduce.12.cloned.1.call-update) | async-done | bytes 524304 | tf_op jit(solution)/shard_map/psum | solution.py:122
  1259.4 1.3 fusion.54
  1260.7 1.3 fusion.56
  1262.2 11.4 psum.70
  1273.7 2.4 fusion.104
  1276.1 2.4 fusion.105
  1281.6 80.7 %all-reduce.14.cloned.1.call-done = f32[2,64,3072]{2,1,0:T(8,128)} async-done(((f32[2,64,3072]{2,1,0:T(8,128)}), f32[2,64,3072]{2,1,0:T(8,128)}) %all-reduce.14.cloned.1.call-update) | async-done | bytes 1572880 | tf_op jit(solution)/shard_map/psum | solution.py:133
  1363.4 2.1 collective-permute-start
  1365.6 15.7 %collective-permute-done = f32[2,16,3072]{2,1,0:T(8,128)S(1)} collective-permute-done((f32[2,16,3072]{2,1,0:T(8,128)S(1)}, f32[2,16,3072]{2,1,0:T(8,128)S(1)}, u32[]{:S(2)}, u32[]{:S(2)}) %collective-permute-start) | collective-permute-done | bytes 393248 | tf_op jit(solution)/shard_map/ppermute | solution.py:22
  1382.4 18.0 %fusion.21 = f32[48,1024]{1,0:T(8,128)S(1)} fusion(f32[48,1024]{1,0:T(8,128)S(1)} %reshape_squeeze.7), kind=kOutput, calls=%fused_computation.28 | convolution fusion | flops 618659840 | bytes 393216 | tf_op jit(solution)/shard_map/dot_general | solution.py:59
  1400.5 18.0 %fusion.23 = f32[48,1024]{1,0:T(8,128)S(1)} fusion(f32[48,1024]{1,0:T(8,128)S(1)} %reshape_squeeze.6), kind=kOutput, calls=%fused_computation.29 | convolution fusion | flops 618659840 | bytes 393216 | tf_op jit(solution)/shard_map/dot_general | solution.py:59
  1418.6 18.3 %fusion.38 = f32[48,1024]{1,0:T(8,128)S(1)} fusion(f32[48,1024]{1,0:T(8,128)S(1)} %fusion.21, f32[48,1024]{1,0:T(8,128)S(1)} %reshape_squeeze.6), kind=kOutput, calls=%fused_computation.40 | convolution fusion | flops 618758144 | bytes 589824 | tf_op jit(solution)/shard_map/dot_general | solution.py:59
  1437.0 18.1 %fusion.32 = f32[48,1024]{1,0:T(8,128)S(1)} fusion(f32[48,1024]{1,0:T(8,128)S(1)} %fusion.23, f32[48,1024]{1,0:T(8,128)S(1)} %reshape_squeeze.7), kind=kOutput, calls=%fused_computation.38 | convolution fusion | flops 618758144 | bytes 589824 | tf_op jit(solution)/shard_map/dot_general | solution.py:59
  (87 shorter events, 33.1 us)
Async XLA Ops:
  7.2 1.9 copy-start.1
  7.2 226.6 %all-gather.2.cloned.1.call-start = ((), (), s32[]{:S(2)}) async-start(), calls=%async_computation | async-start | bytes 15728640 | tf_op jit(solution)/shard_map/all_gather | solution.py:100
  7.9 1007.5 %all-reduce.6.cloned.1.call-start = ((), (), s32[]{:S(2)}) async-start(), calls=%async_computation.1 | async-start | bytes 2097152 | tf_op jit(solution)/shard_map/psum | solution.py:102
  265.5 1.4 copy-start.4
  266.8 844.1 %all-reduce.8.cloned.1.call-start = ((), (), s32[]{:S(2)}) async-start(), calls=%async_computation.2 | async-start | bytes 1048576 | tf_op jit(solution)/shard_map/psum | solution.py:122
  1015.4 95.5 %copy-start = (f32[4,128,512]{2,1,0:T(8,128)S(1)}, f32[4,128,512]{2,1,0:T(8,128)}, u32[]{:S(2)}) copy-start(f32[4,128,512]{2,1,0:T(8,128)} %all-reduce.6.cloned.1.call-done) | copy-start | bytes 3145732
  1026.5 157.2 %all-reduce.10.cloned.1.call-start = ((), (), s32[]{:S(2)}) async-start(), calls=%async_computation.3 | async-start | bytes 1048576 | tf_op jit(solution)/shard_map/psum | solution.py:122
  1132.3 123.5 %all-reduce.12.cloned.1.call-start = ((), (), s32[]{:S(2)}) async-start(), calls=%async_computation.4 | async-start | bytes 1048576 | tf_op jit(solution)/shard_map/psum | solution.py:122
  1204.6 157.8 %all-reduce.14.cloned.1.call-start = ((), (), s32[]{:S(2)}) async-start(), calls=%async_computation.5 | async-start | bytes 3145728 | tf_op jit(solution)/shard_map/psum | solution.py:133
  1262.0 16.4 %copy-start.2 = (f32[2,128,3072]{2,1,0:T(8,128)S(1)}, f32[2,128,3072]{2,1,0:T(8,128)}, u32[]{:S(2)}) copy-start(f32[2,128,3072]{2,1,0:T(8,128)} %param.4) | copy-start | bytes 9437188
  1273.7 6.7 copy-start.3
  1279.4 86.1 %copy-start.5 = (s32[4,1024]{1,0:T(4,128)S(1)}, s32[4,1024]{1,0:T(4,128)}, u32[]{:S(2)}) copy-start(s32[4,1024]{1,0:T(4,128)} %param.7) | copy-start | bytes 49156
  1363.4 17.9 %collective-permute-start = (f32[2,16,3072]{2,1,0:T(8,128)S(1)}, f32[2,16,3072]{2,1,0:T(8,128)S(1)}, u32[]{:S(2)}, u32[]{:S(2)}) collective-permute-start(f32[2,16,3072]{2,1,0:T(8,128)S(1)} %constant_dynamic-slice_fusion), channel_id=1, source_target_pairs={{0,4},{4,8},{8,12},{12,16},{16,20},{20,24},{24,28},{28,32},{32,36}... | collective-permute-start | bytes 1179656 | tf_op jit(solution)/shard_map/ppermute | solution.py:22
Sparse Core Ops, SparseCore 0:
  9.8 223.9 all-gather.1
  266.9 748.4 all-reduce.5
  1026.6 84.2 all-reduce.7
  1132.5 51.1 all-reduce.9
  1204.7 51.0 all-reduce.11
  1281.8 80.5 all-reduce.13
where the time goes:
time: 1480 us; the launch traced here: 1460 us
  waiting for transfers between devices  1240 us (84%)
  matrix products  133 us (9%)
  blocking collectives  43.8 us (3%)
  local copies, waits for them, and re-layouts  16.3 us (1%)
  between operations  15.7 us (1%)
    psum x1, waiting for transfers between devices, body(): summed_corr = lax.psum(partial_corr, 'tm')  739 us
    all_gather x1, waiting for transfers between devices, body(): lax.all_gather(samples, 'elem', axis=1, tiled=True)  221 us
    psum x3, waiting for transfers between devices, body(): lax.psum(jnp.stack([adj_real, adj_imag, herm_real, herm_imag]), 'elem')  187 us
    dot_general x16, matrix products, matmul(): jnp.dot(left_rows, right_rows, precision=HIGH, preferred_element_type=jnp...  88.1 us
    psum x1, waiting for transfers between devices, body(): beam_all = lax.psum(beam_partial, 'elem')  80.7 us
    psum x4, blocking collectives, column_norms(): return lax.psum(column_squares(vector), 'elem')  43.8 us
  transfers between devices with their start and end apart: 7, of which 7 were waited for; matrix products, arithmetic and copies ran while one was open for 0% of the time, Pallas kernels for 0%

commit v1 on v0

v1 whole, which is shorter than its diff:
```python
import functools
import math

import jax
import jax.numpy as jnp
import ml_dtypes
import numpy as np
from jax import lax
from jax.experimental import pallas as pl
from jax.experimental.pallas import tpu as pltpu
from jax.sharding import PartitionSpec as P

ELEMS = 512
BEAMS = 64
CHANNELS = 1024
TAPS = 4
ITERS = 3
SPAN = 3072
SAMPLES = 196608
FRAMES = SPAN // CHANNELS
GROUP = 4
OWN = ELEMS // GROUP
PART = CHANNELS // GROUP
TM = SAMPLES // SPAN
QUARTER = BEAMS // GROUP

EPS = 1e-06
F32 = jnp.float32
BF16 = jnp.bfloat16
MESH = pl.DeviceIdType.MESH
VMEM_LIMIT = 56 * 1024 * 1024

CORR_ROWS = 3 * 4 * ELEMS
HALF = CORR_ROWS // 2
SEG = HALF // 3
AXIS_SIZE = {"x": 4, "y": 4, "z": 8}
ORDERS = (("x", "y", "z"), ("y", "z", "x"), ("z", "x", "y"))


def split(value):
    high = value.astype(BF16)
    return high, (value - high.astype(F32)).astype(BF16)


def dot_nt(left, right):
    return lax.dot_general(left, right, (((1,), (1,)), ((), ())), preferred_element_type=F32)


def dot_nn(left, right):
    return lax.dot_general(left, right, (((1,), (0,)), ((), ())), preferred_element_type=F32)


def cat(*pieces):
    return jnp.concatenate(pieces, axis=1)


def corr_kernel(x_ref, start_ref, cos_ref, sin_ref, x_out, start_out, g_ref, xg, sg, rh, rl, uh, ul,
                send_sem, recv_sem, own_sem, out_sem, s_send, s_recv):
    me = lax.axis_index("elem")
    barrier = pltpu.get_barrier_semaphore()
    for off in range(1, GROUP):
        pl.semaphore_signal(barrier, inc=1, device_id={"elem": lax.rem(me + off, GROUP)}, device_id_type=MESH)
    pl.semaphore_wait(barrier, GROUP - 1)

    def start_copy(off):
        peer = lax.rem(me + off, GROUP)
        return pltpu.make_async_remote_copy(
            src_ref=start_ref, dst_ref=sg.at[pl.ds(pl.multiple_of(me * OWN, OWN), OWN), :],
            send_sem=s_send.at[off], recv_sem=s_recv.at[off], device_id={"elem": peer}, device_id_type=MESH)

    def sample_copy(frame, off):
        peer = lax.rem(me + off, GROUP)
        col = pl.multiple_of(frame * CHANNELS + peer * PART, PART)
        return pltpu.make_async_remote_copy(
            src_ref=x_ref.at[:, :, pl.ds(col, PART)],
            dst_ref=xg.at[frame, :, pl.ds(pl.multiple_of(me * OWN, OWN), OWN), :],
            send_sem=send_sem.at[frame, off], recv_sem=recv_sem.at[frame, off],
            device_id={"elem": peer}, device_id_type=MESH)

    def own_copy(frame):
        col = pl.multiple_of(frame * CHANNELS + me * PART, PART)
        return pltpu.make_async_copy(
            x_ref.at[:, :, pl.ds(col, PART)],
            xg.at[frame, :, pl.ds(pl.multiple_of(me * OWN, OWN), OWN), :], own_sem.at[frame])

    def out_copy(frame):
        return pltpu.make_async_copy(xg.at[frame], x_out.at[frame], out_sem.at[frame])

    for frame in range(FRAMES):
        for off in (2, 1, 3):
            sample_copy(frame, off).start()
        own_copy(frame).start()
    for off in range(1, GROUP):
        start_copy(off).start()
    sg[pl.ds(pl.multiple_of(me * OWN, OWN), OWN), :] = start_ref[...]
    g_ref[...] = jnp.zeros_like(g_ref)

    def one_frame(frame, carry):
        own_copy(frame).wait()
        for off in range(1, GROUP):
            sample_copy(frame, off).wait_recv()
        out_copy(frame).start()
        cos_row = cos_ref[pl.ds(frame, 1), :]
        sin_row = sin_ref[pl.ds(frame, 1), :]

        def prepare(block, carry2):
            rows = pl.ds(pl.multiple_of(block * 128, 128), 128)
            real = xg[frame, 0, rows, :]
            imag = xg[frame, 1, rows, :]
            high, low = split(cat(real, imag))
            rh[rows, :] = high
            rl[rows, :] = low
            high, low = split(cat(real * cos_row + imag * sin_row, imag * cos_row - real * sin_row))
            uh[rows, :] = high
            ul[rows, :] = low
            return carry2

        lax.fori_loop(0, 4, prepare, 0)
        right = cat(rh[...], rl[...], rh[...])

        def left_of(high_ref, low_ref, rows, imag):
            high = high_ref[rows, :]
            low = low_ref[rows, :]
            if imag:
                high = cat(high[:, PART:], -high[:, :PART])
                low = cat(low[:, PART:], -low[:, :PART])
            return cat(high, high, low)

        def cyclic(block, carry2):
            rows = pl.ds(pl.multiple_of(block * 256, 256), 256)
            for imag in (0, 1):
                out = dot_nt(left_of(uh, ul, rows, imag), right)
                for col in range(4):
                    g_ref[1 + imag, col, rows, :] += out[:, col * 128:(col + 1) * 128]
            return carry2

        lax.fori_loop(0, 2, cyclic, 0)
        upper = lax.broadcasted_iota(jnp.int32, (256, 256), 0) <= lax.broadcasted_iota(jnp.int32, (256, 256), 1)
        top = pl.ds(0, 256)
        bottom = pl.ds(256, 256)
        out = dot_nt(left_of(rh, rl, top, 0), right)
        diag = jnp.where(upper, out[:, :256], dot_nt(left_of(rh, rl, top, 1), right[:256]))
        g_ref[0, 0, top, :] += diag[:, :128]
        g_ref[0, 1, top, :] += diag[:, 128:]
        g_ref[0, 2, top, :] += out[:, 256:384]
        g_ref[0, 3, top, :] += out[:, 384:]
        out = dot_nt(left_of(rh, rl, bottom, 1), right)
        diag = jnp.where(upper, dot_nt(left_of(rh, rl, bottom, 0), right[256:]), out[:, 256:])
        g_ref[0, 0, bottom, :] += out[:, :128]
        g_ref[0, 1, bottom, :] += out[:, 128:256]
        g_ref[0, 2, bottom, :] += diag[:, :128]
        g_ref[0, 3, bottom, :] += diag[:, 128:]
        return carry

    lax.fori_loop(0, FRAMES, one_frame, 0)
    for off in range(1, GROUP):
        start_copy(off).wait()
    start_out[...] = sg[...]
    for frame in range(FRAMES):
        out_copy(frame).wait()
        for off in range(1, GROUP):
            sample_copy(frame, off).wait_send()


def gather_and_correlate(samples, start, cos_rows, sin_rows):
    vmem = pl.BlockSpec(memory_space=pltpu.VMEM)
    hbm = pl.BlockSpec(memory_space=pl.ANY)
    return pl.pallas_call(
        corr_kernel,
        out_shape=(
            jax.ShapeDtypeStruct((FRAMES, 2, ELEMS, PART), F32),
            jax.ShapeDtypeStruct((ELEMS, 2 * BEAMS), F32),
            jax.ShapeDtypeStruct((3, 4, ELEMS, 128), F32),
        ),
        in_specs=[hbm, vmem, vmem, vmem],
        out_specs=(hbm, vmem, vmem),
        scratch_shapes=[
            pltpu.VMEM((FRAMES, 2, ELEMS, PART), F32),
            pltpu.VMEM((ELEMS, 2 * BEAMS), F32),
            pltpu.VMEM((ELEMS, 2 * PART), BF16),
            pltpu.VMEM((ELEMS, 2 * PART), BF16),
            pltpu.VMEM((ELEMS, 2 * PART), BF16),
            pltpu.VMEM((ELEMS, 2 * PART), BF16),
            pltpu.SemaphoreType.DMA((FRAMES, GROUP)),
            pltpu.SemaphoreType.DMA((FRAMES, GROUP)),
            pltpu.SemaphoreType.DMA((FRAMES,)),
            pltpu.SemaphoreType.DMA((FRAMES,)),
            pltpu.SemaphoreType.DMA((GROUP,)),
            pltpu.SemaphoreType.DMA((GROUP,)),
        ],
        compiler_params=pltpu.CompilerParams(
            collective_id=0, has_side_effects=True, vmem_limit_bytes=VMEM_LIMIT),
        name="gather_correlate",
    )(samples, start, cos_rows, sin_rows)


def place():
    tm = lax.axis_index("tm")
    elem = lax.axis_index("elem")
    core = lax.rem(tm, 2)
    return {
        "core": core,
        "x": lax.rem(tm // 2, 4),
        "y": tm // 16,
        "z": lax.rem(tm // 8, 2) * 4 + elem,
    }


def device_at(spot, axis, value):
    at = dict(spot)
    at[axis] = value
    tm = ((at["y"] * 2 + at["z"] // 4) * 4 + at["x"]) * 2 + at["core"]
    return {"tm": tm, "elem": lax.rem(at["z"], 4)}


def reduce_kernel(g_ref, o_ref, w_ref, c_ref, *refs):
    slots = refs[:9]
    core_send, core_recv, rs_send, rs_recv, ag_send, ag_recv = refs[9:]
    spot = place()
    barrier = pltpu.get_barrier_semaphore()
    count = 0
    for axis, size in (("core", 2), ("x", 4), ("y", 4), ("z", 8)):
        for off in range(1, size):
            pl.semaphore_signal(
                barrier, inc=1, device_id=device_at(spot, axis, lax.rem(spot[axis] + off, size)),
                device_id_type=MESH)
            count += 1
    pl.semaphore_wait(barrier, count)

    core = spot["core"]
    sibling = device_at(spot, "core", 1 - core)

    def core_rs(part):
        rows = pl.ds(pl.multiple_of((1 - core) * HALF + part * SEG, SEG), SEG)
        return pltpu.make_async_remote_copy(
            src_ref=g_ref.at[rows, :], dst_ref=c_ref.at[pl.ds(part * SEG, SEG), :],
            send_sem=core_send.at[part], recv_sem=core_recv.at[part], device_id=sibling, device_id_type=MESH)

    for part in (2, 0, 1):
        core_rs(part).start()

    def index(part, stage, off):
        return part * 24 + stage * 8 + off

    def lengths(part):
        out = [SEG]
        for axis in ORDERS[part]:
            out.append(out[-1] // AXIS_SIZE[axis])
        return out

    starts = [[part * SEG] for part in range(3)]
    for part in range(3):
        for stage, axis in enumerate(ORDERS[part]):
            starts[part].append(starts[part][-1] + spot[axis] * lengths(part)[stage + 1])

    def rs_copy(part, stage, off):
        axis = ORDERS[part][stage]
        size = AXIS_SIZE[axis]
        length = lengths(part)[stage + 1]
        peer = lax.rem(spot[axis] + off, size)
        source = pl.multiple_of(starts[part][stage] + peer * length, 8)
        return pltpu.make_async_remote_copy(
            src_ref=w_ref.at[pl.ds(source, length), :],
            dst_ref=slots[part * 3 + stage].at[off],
            send_sem=rs_send.at[index(part, stage, off)], recv_sem=rs_recv.at[index(part, stage, off)],
            device_id=device_at(spot, axis, peer), device_id_type=MESH)

    def ag_copy(part, stage, off):
        axis = ORDERS[part][stage]
        size = AXIS_SIZE[axis]
        length = lengths(part)[stage + 1]
        peer = lax.rem(spot[axis] + off, size)
        where = pl.ds(pl.multiple_of(core * HALF + starts[part][stage + 1], 8), length)
        return pltpu.make_async_remote_copy(
            src_ref=o_ref.at[where, :], dst_ref=o_ref.at[where, :],
            send_sem=ag_send.at[index(part, stage, off)], recv_sem=ag_recv.at[index(part, stage, off)],
            device_id=device_at(spot, axis, peer), device_id_type=MESH)

    def core_ag(part):
        rows = pl.ds(pl.multiple_of(core * HALF + part * SEG, SEG), SEG)
        return pltpu.make_async_remote_copy(
            src_ref=o_ref.at[rows, :], dst_ref=o_ref.at[rows, :],
            send_sem=core_send.at[3 + part], recv_sem=core_recv.at[3 + part],
            device_id=sibling, device_id_type=MESH)

    def peers(part, stage):
        return range(1, AXIS_SIZE[ORDERS[part][stage]])

    for part in (2, 0, 1):
        core_rs(part).wait_recv()
        rows = pl.ds(pl.multiple_of(core * HALF + part * SEG, SEG), SEG)
        w_ref[pl.ds(part * SEG, SEG), :] = g_ref[rows, :] + c_ref[pl.ds(part * SEG, SEG), :]
        for off in peers(part, 0):
            rs_copy(part, 0, off).start()
    for stage in range(3):
        for part in (0, 1, 2):
            for off in peers(part, stage):
                rs_copy(part, stage, off).wait_recv()
            length = lengths(part)[stage + 1]
            rows = pl.ds(pl.multiple_of(starts[part][stage + 1], 8), length)
            total = w_ref[rows, :]
            for off in peers(part, stage):
                total = total + slots[part * 3 + stage][off]
            if stage < 2:
                w_ref[rows, :] = total
                for off in peers(part, stage + 1):
                    rs_copy(part, stage + 1, off).start()
            else:
                o_ref[pl.ds(pl.multiple_of(core * HALF + starts[part][3], 8), length), :] = total
                for off in peers(part, 2):
                    ag_copy(part, 2, off).start()
    for stage in (2, 1, 0):
        for part in (0, 1, 2):
            for off in peers(part, stage):
                ag_copy(part, stage, off).wait_recv()
            if stage > 0:
                for off in peers(part, stage - 1):
                    ag_copy(part, stage - 1, off).start()
            else:
                core_ag(part).start()
    for part in range(3):
        core_ag(part).wait_recv()
    for part in range(3):
        core_rs(part).wait_send()
        core_ag(part).wait_send()
        for stage in range(3):
            for off in peers(part, stage):
                rs_copy(part, stage, off).wait_send()
                ag_copy(part, stage, off).wait_send()


def reduce_all(partial):
    vmem = pl.BlockSpec(memory_space=pltpu.VMEM)
    slots = []
    for order in ORDERS:
        length = SEG
        for axis in order:
            length //= AXIS_SIZE[axis]
            slots.append(pltpu.VMEM((AXIS_SIZE[axis], length, 128), F32))
    return pl.pallas_call(
        reduce_kernel,
        out_shape=jax.ShapeDtypeStruct((CORR_ROWS, 128), F32),
        in_specs=[vmem],
        out_specs=vmem,
        scratch_shapes=[
            pltpu.VMEM((HALF, 128), F32),
            pltpu.VMEM((HALF, 128), F32),
            *slots,
            pltpu.SemaphoreType.DMA((6,)),
            pltpu.SemaphoreType.DMA((6,)),
            pltpu.SemaphoreType.DMA((72,)),
            pltpu.SemaphoreType.DMA((72,)),
            pltpu.SemaphoreType.DMA((72,)),
            pltpu.SemaphoreType.DMA((72,)),
        ],
        compiler_params=pltpu.CompilerParams(
            collective_id=1, has_side_effects=True, vmem_limit_bytes=VMEM_LIMIT),
        name="reduce_correlations",
    )(partial.reshape(CORR_ROWS, 128))


def power_kernel(o_ref, start_ref, v_ref, weights_ref, ah, al, bh, bl):
    def wide(index, rows):
        base = index * 4 * ELEMS
        return cat(*[o_ref[pl.ds(base + col * ELEMS + rows, 128), :] for col in range(4)])

    plain_scale = 1.0 / SAMPLES
    cyc_scale = 1.0 / math.sqrt(SAMPLES * ELEMS)

    def full(index):
        return jnp.concatenate([wide(index, rows) for rows in range(0, ELEMS, 128)], axis=0)

    def put(high_ref, low_ref, col, value):
        high, low = split(value)
        high_ref[:, col * ELEMS:(col + 1) * ELEMS] = high
        low_ref[:, col * ELEMS:(col + 1) * ELEMS] = low

    packed = full(0) * plain_scale
    flipped = packed.T
    row_ids = lax.broadcasted_iota(jnp.int32, (ELEMS, ELEMS), 0)
    col_ids = lax.broadcasted_iota(jnp.int32, (ELEMS, ELEMS), 1)
    put(ah, al, 2, jnp.where(row_ids <= col_ids, packed, flipped))
    put(ah, al, 3, jnp.where(row_ids > col_ids, packed, jnp.where(row_ids < col_ids, -flipped, 0.0)))
    cyc_real = full(1) * cyc_scale
    put(ah, al, 0, cyc_real)
    put(bh, bl, 0, cyc_real.T)
    cyc_imag = full(2) * cyc_scale
    put(ah, al, 1, cyc_imag)
    put(bh, bl, 1, -cyc_imag.T)

    lane = lax.broadcasted_iota(jnp.int32, (ELEMS, 2 * BEAMS), 1)

    def turned(vector):
        other = pltpu.roll(vector, BEAMS, 1)
        return jnp.where(lane < BEAMS, -other, other)

    def normalized(vector):
        squares = jnp.sum(vector * vector, axis=0, keepdims=True)
        squares = jnp.broadcast_to(squares, (8, 2 * BEAMS))
        squares = squares + pltpu.roll(squares, BEAMS, 1)
        return vector * (1.0 / jnp.sqrt(squares[:1] + EPS))

    def stacked(vector):
        high, low = split(jnp.concatenate([vector, turned(vector)], axis=0))
        return cat(high, low)

    def product(high, low, right):
        wide_out = dot_nn(high, right)
        return wide_out[:, :2 * BEAMS] + wide_out[:, 2 * BEAMS:] + dot_nn(low, right[:, :2 * BEAMS])

    v_ref[...] = normalized(start_ref[...])

    def step(iteration, carry):
        held = stacked(v_ref[...])
        mid = product(bh[...], bl[...], held)
        right = jnp.concatenate([stacked(mid), held], axis=0)
        v_ref[...] = normalized(product(ah[...], al[...], right))
        return carry

    lax.fori_loop(0, ITERS, step, 0)
    rows = pl.ds(pl.multiple_of(lax.axis_index("elem") * OWN, OWN), OWN)
    mine = v_ref[rows, :]
    weights_ref[0] = mine[:, :BEAMS]
    weights_ref[1] = pltpu.roll(mine, BEAMS, 1)[:, :BEAMS]


def power(total, start):
    vmem = pl.BlockSpec(memory_space=pltpu.VMEM)
    return pl.pallas_call(
        power_kernel,
        out_shape=(
            jax.ShapeDtypeStruct((ELEMS, 2 * BEAMS), F32),
            jax.ShapeDtypeStruct((2, OWN, BEAMS), F32),
        ),
        in_specs=[vmem, vmem],
        out_specs=(vmem, vmem),
        scratch_shapes=[
            pltpu.VMEM((ELEMS, 4 * ELEMS), BF16),
            pltpu.VMEM((ELEMS, 4 * ELEMS), BF16),
            pltpu.VMEM((ELEMS, 2 * ELEMS), BF16),
            pltpu.VMEM((ELEMS, 2 * ELEMS), BF16),
        ],
        compiler_params=pltpu.CompilerParams(vmem_limit_bytes=VMEM_LIMIT),
        name="power_iterations",
    )(total, start)


def dft_tables():
    ids = np.arange(CHANNELS)
    angle = 2.0 * np.pi / CHANNELS * (ids[:, None] * ids[None, :] % CHANNELS)
    out = []
    for table in (np.cos(angle), np.sin(angle)):
        table = (table / math.sqrt(CHANNELS)).astype(np.float32)
        high = table.astype(ml_dtypes.bfloat16)
        out += [high, (table - high.astype(np.float32)).astype(ml_dtypes.bfloat16)]
    return np.stack(out)


def beam_kernel(x_ref, v_ref, tap_ref, table_ref, out_ref, table, own, after, got_own, got_before,
                table_sem, own_send, own_recv, next_send, next_recv):
    tm = lax.axis_index("tm")
    me = lax.axis_index("elem")
    table_copy = pltpu.make_async_copy(table_ref, table, table_sem)
    table_copy.start()
    barrier = pltpu.get_barrier_semaphore()
    for off in range(1, GROUP):
        pl.semaphore_signal(barrier, inc=1, device_id={"elem": lax.rem(me + off, GROUP)}, device_id_type=MESH)

    @pl.when(tm > 0)
    def _():
        for peer in range(GROUP):
            pl.semaphore_signal(barrier, inc=1, device_id={"tm": tm - 1, "elem": peer}, device_id_type=MESH)

    @pl.when(tm < TM - 1)
    def _():
        for peer in range(GROUP):
            pl.semaphore_signal(barrier, inc=1, device_id={"tm": tm + 1, "elem": peer}, device_id_type=MESH)

    vt = v_ref[...].T
    vh, vl = split(vt)
    left = jnp.concatenate([vh, vl], axis=0)
    taps = tap_ref[...].astype(F32) / 2048.0

    beams_real = []
    beams_imag = []
    for frame in range(FRAMES):
        xh, xl = split(cat(x_ref[frame, 0], x_ref[frame, 1]))
        both = dot_nn(left, xh)
        out = both[:2 * BEAMS] + both[2 * BEAMS:] + dot_nn(vh, xl)
        beams_real.append(out[:BEAMS, :PART] + out[BEAMS:, PART:])
        beams_imag.append(out[:BEAMS, PART:] - out[BEAMS:, :PART])
    for kind, beams in enumerate((beams_real, beams_imag)):
        for frame in range(2 * FRAMES):
            total = None
            for tap in range(TAPS):
                if 0 <= frame - tap < FRAMES:
                    term = taps[tap:tap + 1, :] * beams[frame - tap]
                    total = term if total is None else total + term
            if frame < FRAMES:
                own[kind, frame] = total
            else:
                after[kind, frame - FRAMES] = total

    pl.semaphore_wait(
        barrier, GROUP - 1 + GROUP * ((tm > 0).astype(jnp.int32) + (tm < TM - 1).astype(jnp.int32)))

    def next_copy(off):
        peer = lax.rem(me + off, GROUP)
        rows = pl.ds(pl.multiple_of(peer * QUARTER, QUARTER), QUARTER)
        return pltpu.make_async_remote_copy(
            src_ref=after.at[:, :, rows, :], dst_ref=got_before.at[me],
            send_sem=next_send.at[off], recv_sem=next_recv.at[off],
            device_id={"tm": tm + 1, "elem": peer}, device_id_type=MESH)

    def own_copy(off):
        peer = lax.rem(me + off, GROUP)
        rows = pl.ds(pl.multiple_of(peer * QUARTER, QUARTER), QUARTER)
        return pltpu.make_async_remote_copy(
            src_ref=own.at[:, :, rows, :], dst_ref=got_own.at[me],
            send_sem=own_send.at[off], recv_sem=own_recv.at[off],
            device_id={"elem": peer}, device_id_type=MESH)

    @pl.when(tm < TM - 1)
    def _():
        for off in range(GROUP):
            next_copy(off).start()

    for off in (2, 1, 3):
        own_copy(off).start()
    got_own[me] = own[:, :, pl.ds(pl.multiple_of(me * QUARTER, QUARTER), QUARTER), :]
    for off in range(1, GROUP):
        own_copy(off).wait_recv()

    @pl.when(tm > 0)
    def _():
        for off in range(GROUP):
            next_copy(off).wait_recv()
        got_own[...] = got_own[...] + got_before[...]

    table_copy.wait()
    rows = 2 * FRAMES * QUARTER
    wide = cat(*[got_own[part].reshape(rows, PART) for part in range(GROUP)])
    high, low = split(wide)
    left = jnp.concatenate([high, low], axis=0)

    def times(index):
        both = dot_nn(left, table[index])
        return both[:rows] + both[rows:] + dot_nn(high, table[index + 1])

    with_cos = times(0)
    with_sin = times(2)
    half = FRAMES * QUARTER
    out_ref[0] = with_cos[:half] + with_sin[half:]
    out_ref[1] = with_cos[half:] - with_sin[:half]
    for off in range(1, GROUP):
        own_copy(off).wait_send()

    @pl.when(tm < TM - 1)
    def _():
        for off in range(GROUP):
            next_copy(off).wait_send()


def beamform(x_all, vectors, taps, table):
    vmem = pl.BlockSpec(memory_space=pltpu.VMEM)
    hbm = pl.BlockSpec(memory_space=pl.ANY)
    return pl.pallas_call(
        beam_kernel,
        out_shape=jax.ShapeDtypeStruct((2, FRAMES * QUARTER, CHANNELS), F32),
        in_specs=[vmem, vmem, vmem, hbm],
        out_specs=vmem,
        scratch_shapes=[
            pltpu.VMEM((4, CHANNELS, CHANNELS), BF16),
            pltpu.VMEM((2, FRAMES, BEAMS, PART), F32),
            pltpu.VMEM((2, FRAMES, BEAMS, PART), F32),
            pltpu.VMEM((GROUP, 2, FRAMES, QUARTER, PART), F32),
            pltpu.VMEM((GROUP, 2, FRAMES, QUARTER, PART), F32),
            pltpu.SemaphoreType.DMA,
            pltpu.SemaphoreType.DMA((GROUP,)),
            pltpu.SemaphoreType.DMA((GROUP,)),
            pltpu.SemaphoreType.DMA((GROUP,)),
            pltpu.SemaphoreType.DMA((GROUP,)),
        ],
        compiler_params=pltpu.CompilerParams(
            collective_id=2, has_side_effects=True, vmem_limit_bytes=VMEM_LIMIT),
        name="beams_transform",
    )(x_all, vectors, taps, table)


def body(samples, shift_bin, start_vectors, tap_table):
    me = lax.axis_index("elem")
    frame_ids = lax.broadcasted_iota(jnp.int32, (FRAMES, PART), 0)
    chan_ids = lax.broadcasted_iota(jnp.int32, (FRAMES, PART), 1)
    times = lax.axis_index("tm") * SPAN + frame_ids * CHANNELS + me * PART + chan_ids
    folded = shift_bin[0] * times % SAMPLES
    angle = 2.0 * math.pi / SAMPLES * folded.astype(F32)
    start = jnp.concatenate([start_vectors[0], start_vectors[1]], axis=1).astype(F32) - 4.5
    x_all, start_all, partial = gather_and_correlate(samples, start, jnp.cos(angle), jnp.sin(angle))
    total = reduce_all(partial)
    vectors, weights = power(total, start_all)
    taps = lax.dynamic_slice_in_dim(tap_table, me * PART, PART, 1)
    spectra = beamform(x_all, vectors, taps, jnp.asarray(dft_tables()))
    spectra = spectra.reshape(2, FRAMES, QUARTER, CHANNELS).transpose(0, 2, 1, 3)
    return (spectra, weights)


def solution(mesh):
    return jax.shard_map(
        body,
        mesh=mesh,
        in_specs=(P(None, "elem", "tm"), P(), P(None, "elem", None), P()),
        out_specs=(P(None, "elem", "tm", None), P(None, "elem", None)),
        check_vma=False,
    )
```

time: 1480 us -> 186 us (0.13)
  waiting for transfers between devices: 1240 us -> 0 us
  Pallas kernels: 0 us -> 176 us
  matrix products: 133 us -> 0 us
  blocking collectives: 43.8 us -> 0 us
    psum x5 -> x0, waiting for transfers between devices: 1010 us -> none  [the longest x1 739 us: body(): summed_corr = lax.psum(partial_corr, 'tm')]
    all_gather x1 -> x0, waiting for transfers between devices: 221 us -> none  [body(): lax.all_gather(samples, 'elem', axis=1, tiled=True)]
    pallas_call x0 -> x4, Pallas kernels: none -> 176 us  [the longest x1 81.4 us: gather_and_correlate(): pl.pallas_call(corr_kernel, out_shape=(jax.ShapeDtypeStruct((FRAMES, 2, E...]
    dot_general x45 -> x0, matrix products: 133 us -> none  [the longest x16 88.1 us: matmul(): jnp.dot(left_rows, right_rows, precision=HIGH, preferred_element_type=jnp...]
    psum x4 -> x0, blocking collectives: 43.8 us -> none  [column_norms(): return lax.psum(column_squares(vector), 'elem')]
    ppermute x1 -> x0, waiting for transfers between devices: 15.7 us -> none  [from_behind(): return lax.ppermute(x, axis, pairs)]
  transfers between devices with their start and end apart: 7 -> 0, of which waited for: 7 -> 0; matrix products, arithmetic and copies ran while one was open for 0% -> 0% of each run, Pallas kernels for 0% -> 0%
where the time goes in v1:
time: 186 us; the launch traced here: 183 us
  Pallas kernels  176 us (95%)
  local copies, waits for them, and re-layouts  4.05 us (2%)
    pallas_call x1, Pallas kernels, gather_and_correlate(): pl.pallas_call(corr_kernel, out_shape=(jax.ShapeDtypeStruct((FRAMES, 2, E...  81.4 us
    pallas_call x1, Pallas kernels, reduce_all(): pl.pallas_call(reduce_kernel, out_shape=jax.ShapeDtypeStruct((CORR_ROWS,...  58 us
    pallas_call x1, Pallas kernels, beamform(): pl.pallas_call(beam_kernel, out_shape=jax.ShapeDtypeStruct((2, FRAMES * Q...  26.9 us
    pallas_call x1, Pallas kernels, power(): pl.pallas_call(power_kernel, out_shape=(jax.ShapeDtypeStruct((ELEMS, 2 *...  9.98 us

profile of v1, /device:TPU:40, one launch (start us, length us, event | category | flops | bytes accessed | tf_op | source)
XLA Modules:
  0.0 183.1 jit_solution(8840561392249868639)
XLA Ops:
  0.6 0.0 copy-start
  1.3 0.7 fusion.6
  2.0 0.8 fusion.8
  2.8 0.1 copy.10
  2.9 0.1 copy.11
  3.0 0.7 fusion.start_ref
  3.7 81.4 %gather_correlate.1 = (f32[3,2,512,256]{3,2,1,0:T(8,128)}, f32[512,128]{1,0:T(8,128)}, f32[3,4,512,128]{3,2,1,0:T(8,128)}) custom-call(f32[2,128,3072]{2,1,0:T(8,128)} %x_ref.1, f32[128,128]{1,0:T(8,128)} %fusion.start_ref, f32[3,256]{1,0:T(4,128)} %get-tuple-element.17.cos_ref, f32[3,256]{1,0:T(4,128)} %get-tuple-element.16.sin_ref), custom_call_target="tpu_custom_call" | custom-call | tf_op jit(solution)/shard_map/gather_correlate/pallas_call | solution.py:168
  85.1 58.0 %reduce_correlations.1.o_ref = f32[6144,128]{1,0:T(8,128)} custom-call(f32[6144,128]{1,0:T(8,128)} %bitcast.8), custom_call_target="tpu_custom_call" | custom-call | tf_op jit(solution)/shard_map/reduce_correlations/pallas_call | solution.py:340
  143.1 10.0 %power_iterations.1 = (f32[512,128]{1,0:T(8,128)}, f32[2,128,64]{2,1,0:T(8,128)}) custom-call(f32[6144,128]{1,0:T(8,128)} %reduce_correlations.1.o_ref, f32[512,128]{1,0:T(8,128)} %get-tuple-element.9.start_ref), custom_call_target="tpu_custom_call" | custom-call | tf_op jit(solution)/shard_map/power_iterations/pallas_call | solution.py:429
  153.1 0.0 copy-done
  153.1 0.6 constant_dynamic-slice_fusion.tap_ref
  153.7 0.0 copy-start.1
  153.7 26.9 %beams_transform.1 = f32[2,48,1024]{2,1,0:T(8,128)} custom-call(f32[3,2,512,256]{3,2,1,0:T(8,128)} %get-tuple-element.7.x_ref, f32[512,128]{1,0:T(8,128)} %get-tuple-element.10.v_ref, s32[4,256]{1,0:T(4,128)} %constant_dynamic-slice_fusion.tap_ref, bf16[4,1024,1024]{2,1,0:T(8,128)(2,1)} %constant.36.clone.table_ref), custom_call_target="tpu_custom_call" | custom-call | tf_op jit(solution)/shard_map/beams_transform/pallas_call | solution.py:567
  180.6 0.0 copy-done.1
  180.6 0.7 copy.9
  181.3 1.8 copy.14
  (1 shorter events, 0.0 us)
Async XLA Ops:
  0.6 152.5 %copy-start = (s32[4,1024]{1,0:T(4,128)S(1)}, s32[4,1024]{1,0:T(4,128)}, u32[]{:S(2)}) copy-start(s32[4,1024]{1,0:T(4,128)} %param.8) | copy-start | bytes 49156
  153.7 26.9 %copy-start.1 = (f32[2,128,64]{2,1,0:T(8,128)S(1)}, f32[2,128,64]{2,1,0:T(8,128)}, u32[]{:S(2)}) copy-start(f32[2,128,64]{2,1,0:T(8,128)} %get-tuple-element.13) | copy-start | bytes 196612

commit v2 on v0

v2 whole, which is shorter than its diff:
```python
import math

import jax
import jax.numpy as jnp
import ml_dtypes
import numpy as np
from jax import lax
from jax.experimental import pallas as pl
from jax.experimental.pallas import tpu as pltpu
from jax.sharding import PartitionSpec as P

ELEMS = 512
BEAMS = 64
CHANNELS = 1024
TAPS = 4
ITERS = 3
SPAN = 3072
SAMPLES = 196608
FRAMES = SPAN // CHANNELS
GROUP = 4
OWN = ELEMS // GROUP
PART = CHANNELS // GROUP
TM = SAMPLES // SPAN
QUARTER = BEAMS // GROUP

EPS = 1e-06
F32 = jnp.float32
BF16 = jnp.bfloat16
MESH = pl.DeviceIdType.MESH
VMEM_LIMIT = 56 * 1024 * 1024

CHUNK = 128
CHUNKS = SPAN // GROUP // CHUNK
BLOCK = 128
SIZES = {"core": 2, "x": 4, "y": 4, "z": 8}
PLANE = (("x", "y"), ("y", "x"))


def split(value):
    high = value.astype(BF16)
    return high, (value - high.astype(F32)).astype(BF16)


def dot_nt(left, right):
    return lax.dot_general(left, right, (((1,), (1,)), ((), ())), preferred_element_type=F32)


def dot_nn(left, right):
    return lax.dot_general(left, right, (((1,), (0,)), ((), ())), preferred_element_type=F32)


def cat(*pieces):
    return jnp.concatenate(pieces, axis=1)


def dft_tables():
    ids = np.arange(CHANNELS)
    angle = 2.0 * np.pi / CHANNELS * (ids[:, None] * ids[None, :] % CHANNELS)
    out = []
    for table in (np.cos(angle), np.sin(angle)):
        table = (table / math.sqrt(CHANNELS)).astype(np.float32)
        high = table.astype(ml_dtypes.bfloat16)
        out += [high, (table - high.astype(np.float32)).astype(ml_dtypes.bfloat16)]
    return np.stack(out)


def place():
    tm = lax.axis_index("tm")
    return {
        "core": lax.rem(tm, 2),
        "x": lax.rem(tm // 2, 4),
        "y": tm // 16,
        "z": lax.rem(tm // 8, 2) * 4 + lax.axis_index("elem"),
    }


def device_at(spot, axis, value):
    at = dict(spot)
    at[axis] = value
    tm = ((at["y"] * 2 + at["z"] // 4) * 4 + at["x"]) * 2 + at["core"]
    return {"tm": tm, "elem": lax.rem(at["z"], 4)}


def aligned(start, size):
    return pl.ds(pl.multiple_of(start, size), size)


def kernel(x_ref, start_ref, shift_ref, tap_ref, table_ref, out_ref, weights_ref,
           xg, sg, phase, rh, rl, uh, ul, g, o, pair_got, first_got, second_got, z_got, v_ref, ah, al, bh, bl,
           table, own, after, halo, got, crossed,
           send_sem, recv_sem, own_sem, s_send, s_recv, table_sem,
           pair_send, pair_recv, rs_send, rs_recv, z_send, z_recv, az_send, az_recv, ag_send, ag_recv,
           fw_send, fw_recv, halo_send, halo_recv, cross_send, cross_recv, last_send, last_recv):
    tm = lax.axis_index("tm")
    me = lax.axis_index("elem")
    spot = place()
    core = spot["core"]

    table_copy = pltpu.make_async_copy(table_ref, table, table_sem)
    table_copy.start()

    barrier = pltpu.get_barrier_semaphore()
    count = 0
    for axis, size in SIZES.items():
        for off in range(1, size):
            pl.semaphore_signal(
                barrier, inc=1, device_id=device_at(spot, axis, lax.rem(spot[axis] + off, size)),
                device_id_type=MESH)
            count += 1
    turn = lax.rem(tm, 8)
    near_out = turn != 7
    near_in = turn != 0
    cross_out = jnp.logical_and(turn == 7, tm < TM - 1)
    cross_in = jnp.logical_and(turn == 0, tm > 0)

    @pl.when(near_out)
    def _():
        pl.semaphore_signal(barrier, inc=1, device_id={"tm": tm + 1, "elem": me}, device_id_type=MESH)

    @pl.when(near_in)
    def _():
        pl.semaphore_signal(barrier, inc=1, device_id={"tm": tm - 1, "elem": me}, device_id_type=MESH)

    @pl.when(cross_out)
    def _():
        for peer in range(GROUP):
            pl.semaphore_signal(barrier, inc=1, device_id={"tm": tm + 1, "elem": peer}, device_id_type=MESH)

    @pl.when(cross_in)
    def _():
        for peer in range(GROUP):
            pl.semaphore_signal(barrier, inc=1, device_id={"tm": tm - 1, "elem": peer}, device_id_type=MESH)

    number = lambda flag: flag.astype(jnp.int32)
    pl.semaphore_wait(
        barrier, count + number(near_out) + number(near_in) + GROUP * (number(cross_out) + number(cross_in)))

    def start_copy(off):
        return pltpu.make_async_remote_copy(
            src_ref=sg.at[aligned(me * OWN, OWN), :], dst_ref=sg.at[aligned(me * OWN, OWN), :],
            send_sem=s_send.at[off], recv_sem=s_recv.at[off],
            device_id={"elem": lax.rem(me + off, GROUP)}, device_id_type=MESH)

    def columns(chunk, peer):
        return aligned(chunk // 2 * CHANNELS + peer * PART + lax.rem(chunk, 2) * CHUNK, CHUNK)

    def sample_copy(chunk, off):
        peer = lax.rem(me + off, GROUP)
        return pltpu.make_async_remote_copy(
            src_ref=x_ref.at[:, :, columns(chunk, peer)], dst_ref=xg.at[chunk, :, aligned(me * OWN, OWN), :],
            send_sem=send_sem.at[chunk, off], recv_sem=recv_sem.at[chunk, off],
            device_id={"elem": peer}, device_id_type=MESH)

    def own_copy(chunk):
        return pltpu.make_async_copy(
            x_ref.at[:, :, columns(chunk, me)], xg.at[chunk, :, aligned(me * OWN, OWN), :], own_sem.at[chunk])

    for chunk in range(CHUNKS):
        for off in (2, 1, 3):
            sample_copy(chunk, off).start()
        own_copy(chunk).start()
    sg[aligned(me * OWN, OWN), :] = (start_ref[...].reshape(2 * BEAMS, OWN).astype(F32) - 4.5).T
    for off in range(1, GROUP):
        start_copy(off).start()

    rows8 = lax.broadcasted_iota(jnp.int32, (8, CHUNK), 0)
    lanes = lax.broadcasted_iota(jnp.int32, (8, CHUNK), 1)
    times = tm * SPAN + rows8 // 2 * CHANNELS + me * PART + lax.rem(rows8, 2) * CHUNK + lanes
    turns = (times * shift_ref[0]).astype(F32)
    folded = turns - jnp.floor(turns * (1.0 / SAMPLES)) * SAMPLES
    folded = jnp.where(folded < 0.0, folded + SAMPLES, folded)
    folded = jnp.where(folded >= SAMPLES, folded - SAMPLES, folded)
    angle = 2.0 * math.pi / SAMPLES * folded
    phase[0] = jnp.cos(angle)
    phase[1] = jnp.sin(angle)
    g[...] = jnp.zeros_like(g)

    upper = lax.broadcasted_iota(jnp.int32, (256, 256), 0) <= lax.broadcasted_iota(jnp.int32, (256, 256), 1)

    def left_of(high_ref, low_ref, rows, imag):
        high = high_ref[rows, :]
        low = low_ref[rows, :]
        if imag:
            high = cat(high[:, CHUNK:], -high[:, :CHUNK])
            low = cat(low[:, CHUNK:], -low[:, :CHUNK])
        return cat(high, high, low)

    def add_blocks(kind, first, strip, value):
        for i in range(value.shape[0] // BLOCK):
            for j in range(2):
                row = first + i
                g[(row + j) % 2, strip * 4 + row, kind] += value[
                    i * BLOCK:(i + 1) * BLOCK, j * BLOCK:(j + 1) * BLOCK]

    def arrive(chunk):
        own_copy(chunk).wait()
        for off in range(1, GROUP):
            sample_copy(chunk, off).wait_recv()
        cos_row = phase[0, pl.ds(chunk, 1), :]
        sin_row = phase[1, pl.ds(chunk, 1), :]
        for block in range(4):
            rows = pl.ds(block * BLOCK, BLOCK)
            real = xg[chunk, 0, rows, :]
            imag = xg[chunk, 1, rows, :]
            rh[rows, :], rl[rows, :] = split(cat(real, imag))
            uh[rows, :], ul[rows, :] = split(cat(real * cos_row + imag * sin_row, imag * cos_row - real * sin_row))

    def strip_of(strip):
        cols = pl.ds(strip * 256, 256)
        high = rh[cols, :]
        right = cat(high, rl[cols, :], high)
        every = pl.ds(0, ELEMS)
        for imag in (0, 1):
            add_blocks(1 + imag, 0, strip, dot_nt(left_of(uh, ul, every, imag), right))
        diag = jnp.where(
            upper, dot_nt(left_of(rh, rl, cols, 0), right), dot_nt(left_of(rh, rl, cols, 1), right))
        add_blocks(0, strip * 2, strip, diag)
        other = pl.ds((1 - strip) * 256, 256)
        add_blocks(0, (1 - strip) * 2, strip, dot_nt(left_of(rh, rl, other, 1 - strip), right))

    def one_chunk(chunk, carry):
        arrive(chunk)
        strip_of(0)
        strip_of(1)
        return carry

    lax.fori_loop(0, CHUNKS - 1, one_chunk, 0)

    sibling = device_at(spot, "core", 1 - core)

    def pair_copy(part):
        return pltpu.make_async_remote_copy(
            src_ref=g.at[1 - core, pl.ds(part * 4, 4)], dst_ref=pair_got.at[pl.ds(part * 4, 4)],
            send_sem=pair_send.at[part], recv_sem=pair_recv.at[part], device_id=sibling, device_id_type=MESH)

    def piece(part, stage, first, second):
        if stage == 0:
            return aligned(first * 32, 32)
        return aligned(first * 32 + second * 8, 8)

    def rs_copy(part, stage, off):
        axis = PLANE[part][stage]
        peer = lax.rem(spot[axis] + off, 4)
        first, second = spot[PLANE[part][0]], spot[PLANE[part][1]]
        rows = piece(part, 0, peer, 0) if stage == 0 else piece(part, 1, first, peer)
        dst = (first_got if stage == 0 else second_got).at[part, off]
        return pltpu.make_async_remote_copy(
            src_ref=g.at[core, pl.ds(part * 4, 4), :, rows, :], dst_ref=dst,
            send_sem=rs_send.at[part * 8 + stage * 4 + off], recv_sem=rs_recv.at[part * 8 + stage * 4 + off],
            device_id=device_at(spot, axis, peer), device_id_type=MESH)

    def own_rows(part):
        return piece(part, 1, spot[PLANE[part][0]], spot[PLANE[part][1]])

    def rows_of(z):
        part = z // 4
        plane = (spot["x"] * 32 + spot["y"] * 8) * (1 - part) + (spot["y"] * 32 + spot["x"] * 8) * part
        return aligned(plane, 8)

    def z_copy(off):
        peer = lax.rem(spot["z"] + off, 8)
        return pltpu.make_async_remote_copy(
            src_ref=g.at[core, peer, :, rows_of(peer), :], dst_ref=z_got.at[off],
            send_sem=z_send.at[off], recv_sem=z_recv.at[off],
            device_id=device_at(spot, "z", peer), device_id_type=MESH)

    def az_copy(off):
        mine = spot["z"]
        where = o.at[core, mine, :, rows_of(mine), :]
        return pltpu.make_async_remote_copy(
            src_ref=where, dst_ref=where, send_sem=az_send.at[off], recv_sem=az_recv.at[off],
            device_id=device_at(spot, "z", lax.rem(mine + off, 8)), device_id_type=MESH)

    def ag_copy(part, stage, off):
        axis = PLANE[part][stage]
        peer = lax.rem(spot[axis] + off, 4)
        rows = piece(part, stage, spot[PLANE[part][0]], spot[PLANE[part][1]])
        where = o.at[core, pl.ds(part * 4, 4), :, rows, :]
        return pltpu.make_async_remote_copy(
            src_ref=where, dst_ref=where,
            send_sem=ag_send.at[part * 8 + stage * 4 + off], recv_sem=ag_recv.at[part * 8 + stage * 4 + off],
            device_id=device_at(spot, axis, peer), device_id_type=MESH)

    def forward_copy(part, off):
        origin = lax.rem(spot[PLANE[part][0]] + 4 - off, 4)
        where = o.at[core, pl.ds(part * 4, 4), :, aligned(origin * 32, 32), :]
        return pltpu.make_async_remote_copy(
            src_ref=where, dst_ref=where, send_sem=fw_send.at[part * 4 + off], recv_sem=fw_recv.at[part * 4 + off],
            device_id=sibling, device_id_type=MESH)

    arrive(CHUNKS - 1)
    for part in range(2):
        strip_of(part)
        pair_copy(part).start()
    for part in range(2):
        pair_copy(part).wait_recv()
        for slot in range(part * 4, part * 4 + 4):
            g[core, slot] += pair_got[slot]
        for off in (2, 1, 3):
            rs_copy(part, 0, off).start()
    for part in range(2):
        rows = piece(part, 0, spot[PLANE[part][0]], 0)
        for off in (1, 3, 2):
            rs_copy(part, 0, off).wait_recv()
        g[core, pl.ds(part * 4, 4), :, rows, :] += first_got[part, 1] + first_got[part, 2] + first_got[part, 3]
        for off in (2, 1, 3):
            rs_copy(part, 1, off).start()
    for part in range(2):
        for off in (1, 3, 2):
            rs_copy(part, 1, off).wait_recv()
        g[core, pl.ds(part * 4, 4), :, own_rows(part), :] += (
            second_got[part, 1] + second_got[part, 2] + second_got[part, 3])
    z_order = (4, 3, 5, 2, 6, 1, 7)
    for off in z_order:
        z_copy(off).start()
    mine = spot["z"]
    total = g[core, mine, :, rows_of(mine), :]
    for off in range(1, 8):
        z_copy(off).wait_recv()
    for off in range(1, 8):
        total = total + z_got[off]
    o[core, mine, :, rows_of(mine), :] = total
    for off in z_order:
        az_copy(off).start()
    for off in range(1, 8):
        az_copy(off).wait_recv()
    for part in range(2):
        for off in (2, 1, 3):
            ag_copy(part, 1, off).start()
    for part in range(2):
        for off in (1, 3, 2):
            ag_copy(part, 1, off).wait_recv()
        for off in (2, 1, 3):
            ag_copy(part, 0, off).start()
        forward_copy(part, 0).start()
    for off in (1, 3, 2):
        for part in range(2):
            ag_copy(part, 0, off).wait_recv()
            forward_copy(part, off).start()
    for off in range(1, GROUP):
        start_copy(off).wait_recv()
    for part in range(2):
        for off in range(4):
            forward_copy(part, off).wait_recv()

    plain_scale = 1.0 / SAMPLES
    cyc_scale = 1.0 / math.sqrt(SAMPLES * ELEMS)

    def full(kind):
        return jnp.concatenate(
            [cat(*[o[(i + j) % 2, j // 2 * 4 + i, kind] for j in range(4)]) for i in range(4)], axis=0)

    def put(high_ref, low_ref, col, value):
        high, low = split(value)
        high_ref[:, col * ELEMS:(col + 1) * ELEMS] = high
        low_ref[:, col * ELEMS:(col + 1) * ELEMS] = low

    packed = full(0) * plain_scale
    flipped = packed.T
    row_ids = lax.broadcasted_iota(jnp.int32, (ELEMS, ELEMS), 0)
    col_ids = lax.broadcasted_iota(jnp.int32, (ELEMS, ELEMS), 1)
    put(ah, al, 2, jnp.where(row_ids <= col_ids, packed, flipped))
    put(ah, al, 3, jnp.where(row_ids > col_ids, packed, jnp.where(row_ids < col_ids, -flipped, 0.0)))
    cyc_real = full(1) * cyc_scale
    put(ah, al, 0, cyc_real)
    put(bh, bl, 0, cyc_real.T)
    cyc_imag = full(2) * cyc_scale
    put(ah, al, 1, cyc_imag)
    put(bh, bl, 1, -cyc_imag.T)

    lane = lax.broadcasted_iota(jnp.int32, (ELEMS, 2 * BEAMS), 1)

    def turned(vector):
        other = pltpu.roll(vector, BEAMS, 1)
        return jnp.where(lane < BEAMS, -other, other)

    def normalized(vector):
        squares = jnp.sum(vector * vector, axis=0, keepdims=True)
        squares = jnp.broadcast_to(squares, (8, 2 * BEAMS))
        squares = squares + pltpu.roll(squares, BEAMS, 1)
        return vector * (1.0 / jnp.sqrt(squares[:1] + EPS))

    def stacked(vector):
        high, low = split(jnp.concatenate([vector, turned(vector)], axis=0))
        return cat(high, low)

    def product(high, low, right):
        wide_out = dot_nn(high, right)
        return wide_out[:, :2 * BEAMS] + wide_out[:, 2 * BEAMS:] + dot_nn(low, right[:, :2 * BEAMS])

    v_ref[...] = normalized(sg[...])

    def step(iteration, carry):
        held = stacked(v_ref[...])
        mid = product(bh[...], bl[...], held)
        v_ref[...] = normalized(product(ah[...], al[...], jnp.concatenate([stacked(mid), held], axis=0)))
        return carry

    lax.fori_loop(0, ITERS, step, 0)
    weights_ref[...] = v_ref[aligned(me * OWN, OWN), :].T.reshape(2, BEAMS, OWN)

    vh, vl = split(v_ref[...].T)
    left = jnp.concatenate([vh, vl], axis=0)
    taps = tap_ref[:, aligned(me * PART, PART)].astype(F32) / 2048.0
    beams = ([], [])
    for frame in range(FRAMES):
        pieces = [xg[frame * 2 + half, kind] for kind in range(2) for half in range(2)]
        xh, xl = split(cat(*pieces))
        both = dot_nn(left, xh)
        out = both[:2 * BEAMS] + both[2 * BEAMS:] + dot_nn(vh, xl)
        beams[0].append(out[:BEAMS, :PART] + out[BEAMS:, PART:])
        beams[1].append(out[:BEAMS, PART:] - out[BEAMS:, :PART])

    def filtered(kind, frame):
        total = None
        for tap in range(TAPS):
            if 0 <= frame - tap < FRAMES:
                term = taps[tap:tap + 1, :] * beams[kind][frame - tap]
                total = term if total is None else total + term
        return total

    for kind in range(2):
        for frame in range(FRAMES):
            after[kind, frame] = filtered(kind, frame + FRAMES)

    def quarter(off):
        return aligned(lax.rem(me + off, GROUP) * QUARTER, QUARTER)

    def halo_copy(off):
        rows = quarter(off)
        return pltpu.make_async_remote_copy(
            src_ref=after.at[:, :, rows, :], dst_ref=halo.at[:, :, rows, :],
            send_sem=halo_send.at[off], recv_sem=halo_recv.at[off],
            device_id={"tm": tm + 1, "elem": me}, device_id_type=MESH)

    def cross_copy(off):
        return pltpu.make_async_remote_copy(
            src_ref=after.at[:, :, quarter(off), :], dst_ref=crossed.at[off],
            send_sem=cross_send.at[off], recv_sem=cross_recv.at[off],
            device_id={"tm": tm + 1, "elem": lax.rem(me + off, GROUP)}, device_id_type=MESH)

    def last_copy(off):
        return pltpu.make_async_remote_copy(
            src_ref=own.at[:, :, quarter(off), :], dst_ref=got.at[off],
            send_sem=last_send.at[off], recv_sem=last_recv.at[off],
            device_id={"elem": lax.rem(me + off, GROUP)}, device_id_type=MESH)

    order = (2, 1, 3, 0)

    @pl.when(near_out)
    def _():
        for off in order:
            halo_copy(off).start()

    @pl.when(cross_out)
    def _():
        for off in order:
            cross_copy(off).start()

    for kind in range(2):
        for frame in range(FRAMES):
            own[kind, frame] = filtered(kind, frame)

    for off in order:
        @pl.when(near_in)
        def _():
            halo_copy(off).wait_recv()
            rows = quarter(off)
            own[:, :, rows, :] += halo[:, :, rows, :]

        if off:
            last_copy(off).start()
        else:
            got[0] = own[:, :, quarter(0), :]

    table_copy.wait()
    rows = 2 * FRAMES * QUARTER
    half = FRAMES * QUARTER
    for position, off in enumerate((0, 1, 3, 2)):
        if off:
            last_copy(off).wait_recv()

        @pl.when(cross_in)
        def _():
            cross_copy(off).wait_recv()
            got[off] += crossed[off]

        high, low = split(got[off].reshape(rows, PART))
        left = jnp.concatenate([high, low], axis=0)
        where = aligned(lax.rem(me + GROUP - off, GROUP) * PART, PART)

        def times_table(index):
            both = dot_nn(left, table[index, where, :])
            return both[:rows] + both[rows:] + dot_nn(high, table[index + 1, where, :])

        with_cos = times_table(0)
        with_sin = times_table(2)
        real = with_cos[:half] + with_sin[half:]
        imag = with_cos[half:] - with_sin[:half]
        if position == 0:
            out_ref[0] = real
            out_ref[1] = imag
        else:
            out_ref[0] += real
            out_ref[1] += imag

    for off in range(1, GROUP):
        last_copy(off).wait_send()
        start_copy(off).wait_send()
        for chunk in range(CHUNKS):
            sample_copy(chunk, off).wait_send()
        for part in range(2):
            for stage in range(2):
                rs_copy(part, stage, off).wait_send()
                ag_copy(part, stage, off).wait_send()
    for off in range(1, 8):
        z_copy(off).wait_send()
        az_copy(off).wait_send()
    for part in range(2):
        pair_copy(part).wait_send()
        for off in range(4):
            forward_copy(part, off).wait_send()

    @pl.when(near_out)
    def _():
        for off in order:
            halo_copy(off).wait_send()

    @pl.when(cross_out)
    def _():
        for off in order:
            cross_copy(off).wait_send()


def body(samples, shift_bin, start_vectors, tap_table):
    vmem = pl.BlockSpec(memory_space=pltpu.VMEM)
    smem = pl.BlockSpec(memory_space=pltpu.SMEM)
    hbm = pl.BlockSpec(memory_space=pl.ANY)
    dma = pltpu.SemaphoreType.DMA
    scratch = [
        ((CHUNKS, 2, ELEMS, CHUNK), F32),
        ((ELEMS, 2 * BEAMS), F32),
        ((2, 8, CHUNK), F32),
        ((ELEMS, 2 * CHUNK), BF16),
        ((ELEMS, 2 * CHUNK), BF16),
        ((ELEMS, 2 * CHUNK), BF16),
        ((ELEMS, 2 * CHUNK), BF16),
        ((2, 8, 3, BLOCK, BLOCK), F32),
        ((2, 8, 3, BLOCK, BLOCK), F32),
        ((8, 3, BLOCK, BLOCK), F32),
        ((2, 4, 4, 3, 32, BLOCK), F32),
        ((2, 4, 4, 3, 8, BLOCK), F32),
        ((8, 3, 8, BLOCK), F32),
        ((ELEMS, 2 * BEAMS), F32),
        ((ELEMS, 4 * ELEMS), BF16),
        ((ELEMS, 4 * ELEMS), BF16),
        ((ELEMS, 2 * ELEMS), BF16),
        ((ELEMS, 2 * ELEMS), BF16),
        ((4, CHANNELS, CHANNELS), BF16),
        ((2, FRAMES, BEAMS, PART), F32),
        ((2, FRAMES, BEAMS, PART), F32),
        ((2, FRAMES, BEAMS, PART), F32),
        ((GROUP, 2, FRAMES, QUARTER, PART), F32),
        ((GROUP, 2, FRAMES, QUARTER, PART), F32),
    ]
    semaphores = [
        (CHUNKS, GROUP), (CHUNKS, GROUP), (CHUNKS,), (GROUP,), (GROUP,), None,
        (2,), (2,), (16,), (16,), (8,), (8,), (8,), (8,), (16,), (16,),
        (8,), (8,), (GROUP,), (GROUP,), (GROUP,), (GROUP,), (GROUP,), (GROUP,),
    ]
    spectra, weights = pl.pallas_call(
        kernel,
        out_shape=(
            jax.ShapeDtypeStruct((2, FRAMES * QUARTER, CHANNELS), F32),
            jax.ShapeDtypeStruct((2, BEAMS, OWN), F32),
        ),
        in_specs=[hbm, vmem, smem, vmem, hbm],
        out_specs=(vmem, vmem),
        scratch_shapes=[pltpu.VMEM(*entry) for entry in scratch]
        + [dma if shape is None else dma(shape) for shape in semaphores],
        compiler_params=pltpu.CompilerParams(
            collective_id=0, has_side_effects=True, vmem_limit_bytes=VMEM_LIMIT),
        name="beamformer",
    )(samples, start_vectors.transpose(0, 2, 1), shift_bin, tap_table, jnp.asarray(dft_tables()))
    spectra = spectra.reshape(2, FRAMES, QUARTER, CHANNELS).transpose(0, 2, 1, 3)
    return (spectra, weights.transpose(0, 2, 1))


def solution(mesh):
    return jax.shard_map(
        body,
        mesh=mesh,
        in_specs=(P(None, "elem", "tm"), P(), P(None, "elem", None), P()),
        out_specs=(P(None, "elem", "tm", None), P(None, "elem", None)),
        check_vma=False,
    )
```

time: 1480 us -> 159 us (0.11); the launches traced: 1460 us -> 159 us
  waiting for transfers between devices: 1240 us -> 0 us
  Pallas kernels: 0 us -> 155 us
  matrix products: 133 us -> 0 us
  blocking collectives: 43.8 us -> 0 us
    psum x5 -> x0, waiting for transfers between devices: 1010 us -> none  [the longest x1 739 us: body(): summed_corr = lax.psum(partial_corr, 'tm')]
    all_gather x1 -> x0, waiting for transfers between devices: 221 us -> none  [body(): lax.all_gather(samples, 'elem', axis=1, tiled=True)]
    pallas_call x0 -> x1, Pallas kernels: none -> 155 us  [body(): pl.pallas_call(kernel, out_shape=(jax.ShapeDtypeStruct((2, FRAMES * QUART...]
    dot_general x45 -> x0, matrix products: 133 us -> none  [the longest x16 88.1 us: matmul(): jnp.dot(left_rows, right_rows, precision=HIGH, preferred_element_type=jnp...]
    psum x4 -> x0, blocking collectives: 43.8 us -> none  [column_norms(): return lax.psum(column_squares(vector), 'elem')]
    ppermute x1 -> x0, waiting for transfers between devices: 15.7 us -> none  [from_behind(): return lax.ppermute(x, axis, pairs)]
  transfers between devices with their start and end apart: 7 -> 0, of which waited for: 7 -> 0; matrix products, arithmetic and copies ran while one was open for 0% -> 0% of each run, Pallas kernels for 0% -> 0%
where the time goes in v2:
time: 159 us
  Pallas kernels  155 us (97%)
  local copies, waits for them, and re-layouts  3.24 us (2%)
    pallas_call x1, Pallas kernels, body(): pl.pallas_call(kernel, out_shape=(jax.ShapeDtypeStruct((2, FRAMES * QUART...  155 us
    unnamed x2, local copies, waits for them, and re-layouts  3.24 us

profile of v2, /device:TPU:40, one launch (start us, length us, event | category | flops | bytes accessed | tf_op | source)
XLA Modules:
  0.0 159.1 jit_solution(11466521400058345867)
XLA Ops:
  1.3 154.6 %beamformer.1 = (f32[2,48,1024]{2,1,0:T(8,128)}, f32[2,64,128]{2,1,0:T(8,128)}) custom-call(f32[2,128,3072]{2,1,0:T(8,128)} %x_ref.1, s32[2,64,128]{2,1,0:T(8,128)} %bitcast.6, s32[1]{0:T(128)S(6)} %copy.9.shift_ref, s32[4,1024]{1,0:T(4,128)} %tap_ref.1, bf16[4,1024,1024]{2,1,0:T(8,128)(2,1)} %constant.2.clone.table_ref), custom_call_target="tpu_custom_call" | custom-call | tf_op jit(solution)/shard_map/beamformer/pallas_call | solution.py:571
  155.9 1.8 %copy.10 = f32[2,16,3,1024]{3,1,2,0:T(8,128)} copy(f32[2,16,3,1024]{3,1,2,0:T(8,128)} %bitcast.5) | data formatting | bytes 786432
  157.7 1.5 copy.11

commit v3 on v2

--- a/solution.py
+++ b/solution.py
@@ -85,10 +85,10 @@
     return pl.ds(pl.multiple_of(start, size), size)
 
 
-def kernel(x_ref, start_ref, shift_ref, tap_ref, table_ref, out_ref, weights_ref,
-           xg, sg, phase, rh, rl, uh, ul, g, o, pair_got, first_got, second_got, z_got, v_ref, ah, al, bh, bl,
+def kernel(x_ref, start_hbm, shift_ref, tap_hbm, table_ref, out_ref, weights_ref,
+           start_ref, tap_ref, xg, sg, phase, rh, rl, uh, ul, g, o, pair_got, first_got, second_got, z_got, v_ref, ah, al, bh, bl,
            table, own, after, halo, got, crossed,
-           send_sem, recv_sem, own_sem, s_send, s_recv, table_sem,
+           send_sem, recv_sem, own_sem, s_send, s_recv, table_sem, input_sem,
            pair_send, pair_recv, rs_send, rs_recv, z_send, z_recv, az_send, az_recv, ag_send, ag_recv,
            fw_send, fw_recv, halo_send, halo_recv, cross_send, cross_recv, last_send, last_recv):
     tm = lax.axis_index("tm")
@@ -97,7 +97,10 @@
     core = spot["core"]
 
     table_copy = pltpu.make_async_copy(table_ref, table, table_sem)
-    table_copy.start()
+    start_fetch = pltpu.make_async_copy(start_hbm, start_ref, input_sem.at[0])
+    tap_fetch = pltpu.make_async_copy(tap_hbm, tap_ref, input_sem.at[1])
+    start_fetch.start()
+    tap_fetch.start()
 
     barrier = pltpu.get_barrier_semaphore()
     count = 0
@@ -159,6 +162,8 @@
         for off in (2, 1, 3):
             sample_copy(chunk, off).start()
         own_copy(chunk).start()
+    table_copy.start()
+    start_fetch.wait()
     sg[aligned(me * OWN, OWN), :] = (start_ref[...].reshape(2 * BEAMS, OWN).astype(F32) - 4.5).T
     for off in range(1, GROUP):
         start_copy(off).start()
@@ -333,40 +338,51 @@
         for off in (2, 1, 3):
             ag_copy(part, 0, off).start()
         forward_copy(part, 0).start()
-    for off in (1, 3, 2):
-        for part in range(2):
-            ag_copy(part, 0, off).wait_recv()
-            forward_copy(part, off).start()
-    for off in range(1, GROUP):
-        start_copy(off).wait_recv()
-    for part in range(2):
-        for off in range(4):
-            forward_copy(part, off).wait_recv()
-
     plain_scale = 1.0 / SAMPLES
     cyc_scale = 1.0 / math.sqrt(SAMPLES * ELEMS)
-
-    def full(kind):
-        return jnp.concatenate(
-            [cat(*[o[(i + j) % 2, j // 2 * 4 + i, kind] for j in range(4)]) for i in range(4)], axis=0)
 
     def put(high_ref, low_ref, col, value):
         high, low = split(value)
         high_ref[:, col * ELEMS:(col + 1) * ELEMS] = high
         low_ref[:, col * ELEMS:(col + 1) * ELEMS] = low
 
-    packed = full(0) * plain_scale
+    def prepare(part, off):
+        origin = lax.rem(spot[PLANE[part][0]] + 4 - off, 4)
+        rows = aligned(origin * 32, 32)
+        lanes = aligned(origin * 128, 128)
+        for imag in range(2):
+            for j in (part * 2, part * 2 + 1):
+                slabs = [o[(i + j) % 2, part * 4 + i, 1 + imag, rows, :] * cyc_scale for i in range(4)]
+                slab = jnp.concatenate(slabs, axis=0)
+                high, low = split(slab)
+                cols = pl.ds(imag * ELEMS + j * BLOCK, BLOCK)
+                for i in range(4):
+                    there = aligned(i * BLOCK + origin * 32, 32)
+                    ah[there, cols] = high[i * 32:(i + 1) * 32]
+                    al[there, cols] = low[i * 32:(i + 1) * 32]
+                high, low = split(-slab.T if imag else slab.T)
+                there = pl.ds(imag * ELEMS + pl.multiple_of(origin * 128, 128), 128)
+                bh[j * BLOCK:(j + 1) * BLOCK, there] = high
+                bl[j * BLOCK:(j + 1) * BLOCK, there] = low
+
+    for off in (0, 1, 3, 2):
+        for part in range(2):
+            if off:
+                ag_copy(part, 0, off).wait_recv()
+                forward_copy(part, off).start()
+        for part in range(2):
+            forward_copy(part, off).wait_recv()
+            prepare(part, off)
+    for off in range(1, GROUP):
+        start_copy(off).wait_recv()
+
+    packed = plain_scale * jnp.concatenate(
+        [cat(*[o[(i + j) % 2, j // 2 * 4 + i, 0] for j in range(4)]) for i in range(4)], axis=0)
     flipped = packed.T
     row_ids = lax.broadcasted_iota(jnp.int32, (ELEMS, ELEMS), 0)
     col_ids = lax.broadcasted_iota(jnp.int32, (ELEMS, ELEMS), 1)
     put(ah, al, 2, jnp.where(row_ids <= col_ids, packed, flipped))
     put(ah, al, 3, jnp.where(row_ids > col_ids, packed, jnp.where(row_ids < col_ids, -flipped, 0.0)))
-    cyc_real = full(1) * cyc_scale
-    put(ah, al, 0, cyc_real)
-    put(bh, bl, 0, cyc_real.T)
-    cyc_imag = full(2) * cyc_scale
-    put(ah, al, 1, cyc_imag)
-    put(bh, bl, 1, -cyc_imag.T)
 
     lane = lax.broadcasted_iota(jnp.int32, (ELEMS, 2 * BEAMS), 1)
 
@@ -392,7 +408,10 @@
 
     def step(iteration, carry):
         held = stacked(v_ref[...])
-        mid = product(bh[...], bl[...], held)
+        shuffled = jnp.concatenate(
+            [held[half * ELEMS + i * BLOCK + q * 32:half * ELEMS + i * BLOCK + q * 32 + 32]
+             for half in range(2) for q in range(4) for i in range(4)], axis=0)
+        mid = product(bh[...], bl[...], shuffled)
         v_ref[...] = normalized(product(ah[...], al[...], jnp.concatenate([stacked(mid), held], axis=0)))
         return carry
 
@@ -401,6 +420,7 @@
 
     vh, vl = split(v_ref[...].T)
     left = jnp.concatenate([vh, vl], axis=0)
+    tap_fetch.wait()
     taps = tap_ref[:, aligned(me * PART, PART)].astype(F32) / 2048.0
     beams = ([], [])
     for frame in range(FRAMES):
@@ -532,12 +552,25 @@
             cross_copy(off).wait_send()
 
 
+def finish_kernel(spectra_ref, weights_ref, spectra_out, weights_out, sems):
+    copies = (
+        pltpu.make_async_copy(spectra_ref, spectra_out, sems.at[0]),
+        pltpu.make_async_copy(weights_ref, weights_out, sems.at[1]),
+    )
+    for copy in copies:
+        copy.start()
+    for copy in copies:
+        copy.wait()
+
+
 def body(samples, shift_bin, start_vectors, tap_table):
     vmem = pl.BlockSpec(memory_space=pltpu.VMEM)
     smem = pl.BlockSpec(memory_space=pltpu.SMEM)
     hbm = pl.BlockSpec(memory_space=pl.ANY)
     dma = pltpu.SemaphoreType.DMA
     scratch = [
+        ((2, BEAMS, OWN), jnp.int32),
+        ((TAPS, CHANNELS), jnp.int32),
         ((CHUNKS, 2, ELEMS, CHUNK), F32),
         ((ELEMS, 2 * BEAMS), F32),
         ((2, 8, CHUNK), F32),
@@ -564,7 +597,7 @@
         ((GROUP, 2, FRAMES, QUARTER, PART), F32),
     ]
     semaphores = [
-        (CHUNKS, GROUP), (CHUNKS, GROUP), (CHUNKS,), (GROUP,), (GROUP,), None,
+        (CHUNKS, GROUP), (CHUNKS, GROUP), (CHUNKS,), (GROUP,), (GROUP,), None, (2,),
         (2,), (2,), (16,), (16,), (8,), (8,), (8,), (8,), (16,), (16,),
         (8,), (8,), (GROUP,), (GROUP,), (GROUP,), (GROUP,), (GROUP,), (GROUP,),
     ]
@@ -574,7 +607,7 @@
             jax.ShapeDtypeStruct((2, FRAMES * QUARTER, CHANNELS), F32),
             jax.ShapeDtypeStruct((2, BEAMS, OWN), F32),
         ),
-        in_specs=[hbm, vmem, smem, vmem, hbm],
+        in_specs=[hbm, hbm, smem, hbm, hbm],
         out_specs=(vmem, vmem),
         scratch_shapes=[pltpu.VMEM(*entry) for entry in scratch]
         + [dma if shape is None else dma(shape) for shape in semaphores],
@@ -582,6 +615,17 @@
             collective_id=0, has_side_effects=True, vmem_limit_bytes=VMEM_LIMIT),
         name="beamformer",
     )(samples, start_vectors.transpose(0, 2, 1), shift_bin, tap_table, jnp.asarray(dft_tables()))
+    spectra, weights = pl.pallas_call(
+        finish_kernel,
+        out_shape=(
+            jax.ShapeDtypeStruct((2, FRAMES * QUARTER, CHANNELS), F32),
+            jax.ShapeDtypeStruct((2, BEAMS, OWN), F32),
+        ),
+        in_specs=[hbm, hbm],
+        out_specs=(hbm, hbm),
+        scratch_shapes=[dma((2,))],
+        name="finish",
+    )(spectra, weights)
     spectra = spectra.reshape(2, FRAMES, QUARTER, CHANNELS).transpose(0, 2, 1, 3)
     return (spectra, weights.transpose(0, 2, 1))
 

time: 159 us -> 171 us (1.075)
  Pallas kernels: 155 us -> 170 us
  local copies, waits for them, and re-layouts: 3.24 us -> 0 us
    pallas_call x0 -> x1, Pallas kernels: none -> 15 us  [body(): pl.pallas_call(finish_kernel, out_shape=(jax.ShapeDtypeStruct((2, FRAMES...]
    unnamed x2 -> x0, local copies, waits for them, and re-layouts: 3.24 us -> none
where the time goes in v3:
time: 171 us
  Pallas kernels  170 us (99%)
    pallas_call x1, Pallas kernels, body(): pl.pallas_call(kernel, out_shape=(jax.ShapeDtypeStruct((2, FRAMES * QUART...  155 us
    pallas_call x1, Pallas kernels, body(): pl.pallas_call(finish_kernel, out_shape=(jax.ShapeDtypeStruct((2, FRAMES...  15 us

profile of v3, /device:TPU:40, one launch (start us, length us, event | category | flops | bytes accessed | tf_op | source)
XLA Modules:
  0.0 171.4 jit_solution(8725741608813366243)
XLA Ops:
  1.3 155.1 %beamformer.1 = (f32[2,48,1024]{2,1,0:T(8,128)}, f32[2,64,128]{2,1,0:T(8,128)}) custom-call(f32[2,128,3072]{2,1,0:T(8,128)} %x_ref.1, s32[2,64,128]{2,1,0:T(8,128)} %bitcast.5, s32[1]{0:T(128)S(6)} %copy.7.shift_ref, s32[4,1024]{1,0:T(4,128)} %tap_hbm.1, bf16[4,1024,1024]{2,1,0:T(8,128)(2,1)} %constant.2.clone.table_ref), custom_call_target="tpu_custom_call" | custom-call | tf_op jit(solution)/shard_map/beamformer/pallas_call | solution.py:604
  156.4 15.0 %finish.1 = (f32[2,48,1024]{2,1,0:T(8,128)}, f32[2,64,128]{2,1,0:T(8,128)}) custom-call(f32[2,48,1024]{2,1,0:T(8,128)} %get-tuple-element.6.spectra_ref, f32[2,64,128]{2,1,0:T(8,128)} %get-tuple-element.7.weights_ref), custom_call_target="tpu_custom_call" | custom-call | tf_op jit(solution)/shard_map/finish/pallas_call | solution.py:618

commit v4 on v2

--- a/solution.py
+++ b/solution.py
@@ -30,10 +30,18 @@
 VMEM_LIMIT = 56 * 1024 * 1024
 
 CHUNK = 128
+EARLY = 96
+LATE = OWN - EARLY
+GATE = 4
 CHUNKS = SPAN // GROUP // CHUNK
 BLOCK = 128
 SIZES = {"core": 2, "x": 4, "y": 4, "z": 8}
 PLANE = (("x", "y"), ("y", "x"))
+SLOTS = (
+    ((0, 0), (0, 2), (1, 1), (1, 3), (2, 0), (2, 2), (3, 1), (3, 3)),
+    ((0, 1), (1, 0), (0, 3), (3, 0), (1, 2), (2, 1), (2, 3), (3, 2)),
+)
+SLOT_OF = {block: (parity, slot) for parity in range(2) for slot, block in enumerate(SLOTS[parity])}
 
 
 def split(value):
@@ -85,10 +93,10 @@
     return pl.ds(pl.multiple_of(start, size), size)
 
 
-def kernel(x_ref, start_ref, shift_ref, tap_ref, table_ref, out_ref, weights_ref,
-           xg, sg, phase, rh, rl, uh, ul, g, o, pair_got, first_got, second_got, z_got, v_ref, ah, al, bh, bl,
+def kernel(x_ref, start_hbm, shift_ref, tap_hbm, table_ref, out_ref, weights_ref,
+           start_ref, tap_ref, xg, sg, phase, rh, rl, uh, ul, g, o, pair_got, first_got, second_got, z_got, v_ref, ah, al, bh, bl,
            table, own, after, halo, got, crossed,
-           send_sem, recv_sem, own_sem, s_send, s_recv, table_sem,
+           send_sem, recv_sem, own_sem, s_send, s_recv, table_sem, input_sem,
            pair_send, pair_recv, rs_send, rs_recv, z_send, z_recv, az_send, az_recv, ag_send, ag_recv,
            fw_send, fw_recv, halo_send, halo_recv, cross_send, cross_recv, last_send, last_recv):
     tm = lax.axis_index("tm")
@@ -97,7 +105,10 @@
     core = spot["core"]
 
     table_copy = pltpu.make_async_copy(table_ref, table, table_sem)
-    table_copy.start()
+    start_fetch = pltpu.make_async_copy(start_hbm, start_ref, input_sem.at[0])
+    tap_fetch = pltpu.make_async_copy(tap_hbm, tap_ref, input_sem.at[1])
+    start_fetch.start()
+    tap_fetch.start()
 
     barrier = pltpu.get_barrier_semaphore()
     count = 0
@@ -135,33 +146,49 @@
     pl.semaphore_wait(
         barrier, count + number(near_out) + number(near_in) + GROUP * (number(cross_out) + number(cross_in)))
 
-    def start_copy(off):
-        return pltpu.make_async_remote_copy(
-            src_ref=sg.at[aligned(me * OWN, OWN), :], dst_ref=sg.at[aligned(me * OWN, OWN), :],
-            send_sem=s_send.at[off], recv_sem=s_recv.at[off],
+    firsts = (0, EARLY)
+    counts = (EARLY, LATE)
+
+    def virtual(group):
+        return aligned(me * EARLY, EARLY) if group == 0 else aligned(GROUP * EARLY + me * LATE, LATE)
+
+    def start_copy(group, off):
+        where = sg.at[virtual(group), :]
+        return pltpu.make_async_remote_copy(
+            src_ref=where, dst_ref=where,
+            send_sem=s_send.at[group * 4 + off], recv_sem=s_recv.at[group * 4 + off],
             device_id={"elem": lax.rem(me + off, GROUP)}, device_id_type=MESH)
 
     def columns(chunk, peer):
         return aligned(chunk // 2 * CHANNELS + peer * PART + lax.rem(chunk, 2) * CHUNK, CHUNK)
 
-    def sample_copy(chunk, off):
+    def sample_copy(group, chunk, off):
         peer = lax.rem(me + off, GROUP)
         return pltpu.make_async_remote_copy(
-            src_ref=x_ref.at[:, :, columns(chunk, peer)], dst_ref=xg.at[chunk, :, aligned(me * OWN, OWN), :],
-            send_sem=send_sem.at[chunk, off], recv_sem=recv_sem.at[chunk, off],
+            src_ref=x_ref.at[:, pl.ds(firsts[group], counts[group]), columns(chunk, peer)],
+            dst_ref=xg.at[chunk, :, virtual(group), :],
+            send_sem=send_sem.at[group * CHUNKS + chunk, off], recv_sem=recv_sem.at[group * CHUNKS + chunk, off],
             device_id={"elem": peer}, device_id_type=MESH)
 
-    def own_copy(chunk):
+    def own_copy(group, chunk):
         return pltpu.make_async_copy(
-            x_ref.at[:, :, columns(chunk, me)], xg.at[chunk, :, aligned(me * OWN, OWN), :], own_sem.at[chunk])
-
-    for chunk in range(CHUNKS):
-        for off in (2, 1, 3):
-            sample_copy(chunk, off).start()
-        own_copy(chunk).start()
-    sg[aligned(me * OWN, OWN), :] = (start_ref[...].reshape(2 * BEAMS, OWN).astype(F32) - 4.5).T
-    for off in range(1, GROUP):
-        start_copy(off).start()
+            x_ref.at[:, pl.ds(firsts[group], counts[group]), columns(chunk, me)],
+            xg.at[chunk, :, virtual(group), :], own_sem.at[group * CHUNKS + chunk])
+
+    def send_group(group):
+        for chunk in range(CHUNKS):
+            for off in (2, 1, 3):
+                sample_copy(group, chunk, off).start()
+            own_copy(group, chunk).start()
+
+    send_group(0)
+    table_copy.start()
+    start_fetch.wait()
+    starts = (start_ref[...].reshape(2 * BEAMS, OWN).astype(F32) - 4.5).T
+    for group in range(2):
+        sg[virtual(group), :] = starts[firsts[group]:firsts[group] + counts[group]]
+        for off in range(1, GROUP):
+            start_copy(group, off).start()
 
     rows8 = lax.broadcasted_iota(jnp.int32, (8, CHUNK), 0)
     lanes = lax.broadcasted_iota(jnp.int32, (8, CHUNK), 1)
@@ -175,82 +202,94 @@
     phase[1] = jnp.sin(angle)
     g[...] = jnp.zeros_like(g)
 
-    upper = lax.broadcasted_iota(jnp.int32, (256, 256), 0) <= lax.broadcasted_iota(jnp.int32, (256, 256), 1)
-
-    def left_of(high_ref, low_ref, rows, imag):
-        high = high_ref[rows, :]
-        low = low_ref[rows, :]
+    def triangle(size):
+        return lax.broadcasted_iota(jnp.int32, (size, size), 0) <= lax.broadcasted_iota(jnp.int32, (size, size), 1)
+
+    def left_of(high_ref, low_ref, chunk, rows, imag):
+        high = high_ref[chunk, rows, :]
+        low = low_ref[chunk, rows, :]
         if imag:
             high = cat(high[:, CHUNK:], -high[:, :CHUNK])
             low = cat(low[:, CHUNK:], -low[:, :CHUNK])
         return cat(high, high, low)
 
-    def add_blocks(kind, first, strip, value):
+    def right_of(chunk, rows):
+        high = rh[chunk, rows, :]
+        return cat(high, rl[chunk, rows, :], high)
+
+    def add_blocks(kind, first, first_col, value):
         for i in range(value.shape[0] // BLOCK):
-            for j in range(2):
-                row = first + i
-                g[(row + j) % 2, strip * 4 + row, kind] += value[
-                    i * BLOCK:(i + 1) * BLOCK, j * BLOCK:(j + 1) * BLOCK]
-
-    def arrive(chunk):
-        own_copy(chunk).wait()
+            for j in range(value.shape[1] // BLOCK):
+                parity, slot = SLOT_OF[(first + i, first_col + j)]
+                g[parity, slot, kind] += value[i * BLOCK:(i + 1) * BLOCK, j * BLOCK:(j + 1) * BLOCK]
+
+    def arrive(group, chunk):
+        own_copy(group, chunk).wait()
         for off in range(1, GROUP):
-            sample_copy(chunk, off).wait_recv()
+            sample_copy(group, chunk, off).wait_recv()
         cos_row = phase[0, pl.ds(chunk, 1), :]
         sin_row = phase[1, pl.ds(chunk, 1), :]
-        for block in range(4):
+        for block in ((0, 1, 2), (3,))[group]:
             rows = pl.ds(block * BLOCK, BLOCK)
             real = xg[chunk, 0, rows, :]
             imag = xg[chunk, 1, rows, :]
-            rh[rows, :], rl[rows, :] = split(cat(real, imag))
-            uh[rows, :], ul[rows, :] = split(cat(real * cos_row + imag * sin_row, imag * cos_row - real * sin_row))
-
-    def strip_of(strip):
-        cols = pl.ds(strip * 256, 256)
-        high = rh[cols, :]
-        right = cat(high, rl[cols, :], high)
-        every = pl.ds(0, ELEMS)
+            rh[chunk, rows, :], rl[chunk, rows, :] = split(cat(real, imag))
+            uh[chunk, rows, :], ul[chunk, rows, :] = split(
+                cat(real * cos_row + imag * sin_row, imag * cos_row - real * sin_row))
+
+    front = pl.ds(0, 3 * BLOCK)
+    back = pl.ds(3 * BLOCK, BLOCK)
+
+    def early_chunk(chunk, carry):
+        arrive(0, chunk)
+        right = right_of(chunk, front)
         for imag in (0, 1):
-            add_blocks(1 + imag, 0, strip, dot_nt(left_of(uh, ul, every, imag), right))
-        diag = jnp.where(
-            upper, dot_nt(left_of(rh, rl, cols, 0), right), dot_nt(left_of(rh, rl, cols, 1), right))
-        add_blocks(0, strip * 2, strip, diag)
-        other = pl.ds((1 - strip) * 256, 256)
-        add_blocks(0, (1 - strip) * 2, strip, dot_nt(left_of(rh, rl, other, 1 - strip), right))
-
-    def one_chunk(chunk, carry):
-        arrive(chunk)
-        strip_of(0)
-        strip_of(1)
+            add_blocks(1 + imag, 0, 0, dot_nt(left_of(uh, ul, chunk, front, imag), right))
+        add_blocks(0, 0, 0, jnp.where(
+            triangle(3 * BLOCK), dot_nt(left_of(rh, rl, chunk, front, 0), right),
+            dot_nt(left_of(rh, rl, chunk, front, 1), right)))
         return carry
 
-    lax.fori_loop(0, CHUNKS - 1, one_chunk, 0)
+    def late_chunk(chunk, carry):
+        arrive(1, chunk)
+        right = right_of(chunk, pl.ds(0, ELEMS))
+        last = right_of(chunk, back)
+        for imag in (0, 1):
+            add_blocks(1 + imag, 3, 0, dot_nt(left_of(uh, ul, chunk, back, imag), right))
+            add_blocks(1 + imag, 0, 3, dot_nt(left_of(uh, ul, chunk, front, imag), last))
+        add_blocks(0, 0, 3, dot_nt(left_of(rh, rl, chunk, front, 0), last))
+        low = dot_nt(left_of(rh, rl, chunk, back, 1), right)
+        add_blocks(0, 3, 0, low[:, :3 * BLOCK])
+        add_blocks(0, 3, 3, jnp.where(
+            triangle(BLOCK), dot_nt(left_of(rh, rl, chunk, back, 0), last), low[:, 3 * BLOCK:]))
+        return carry
 
     sibling = device_at(spot, "core", 1 - core)
 
-    def pair_copy(part):
-        return pltpu.make_async_remote_copy(
-            src_ref=g.at[1 - core, pl.ds(part * 4, 4)], dst_ref=pair_got.at[pl.ds(part * 4, 4)],
-            send_sem=pair_send.at[part], recv_sem=pair_recv.at[part], device_id=sibling, device_id_type=MESH)
+    def slots_of(group, part):
+        return pl.ds(part * 4 + group * 2, 2)
+
+    def pair_copy(group, part):
+        return pltpu.make_async_remote_copy(
+            src_ref=g.at[1 - core, slots_of(group, part)], dst_ref=pair_got.at[slots_of(group, part)],
+            send_sem=pair_send.at[group * 2 + part], recv_sem=pair_recv.at[group * 2 + part],
+            device_id=sibling, device_id_type=MESH)
 
     def piece(part, stage, first, second):
         if stage == 0:
             return aligned(first * 32, 32)
         return aligned(first * 32 + second * 8, 8)
 
-    def rs_copy(part, stage, off):
+    def rs_copy(group, part, stage, off):
         axis = PLANE[part][stage]
         peer = lax.rem(spot[axis] + off, 4)
-        first, second = spot[PLANE[part][0]], spot[PLANE[part][1]]
-        rows = piece(part, 0, peer, 0) if stage == 0 else piece(part, 1, first, peer)
-        dst = (first_got if stage == 0 else second_got).at[part, off]
-        return pltpu.make_async_remote_copy(
-            src_ref=g.at[core, pl.ds(part * 4, 4), :, rows, :], dst_ref=dst,
-            send_sem=rs_send.at[part * 8 + stage * 4 + off], recv_sem=rs_recv.at[part * 8 + stage * 4 + off],
+        rows = piece(part, 0, peer, 0) if stage == 0 else piece(part, 1, spot[PLANE[part][0]], peer)
+        index = group * 16 + part * 8 + stage * 4 + off
+        return pltpu.make_async_remote_copy(
+            src_ref=g.at[core, slots_of(group, part), :, rows, :],
+            dst_ref=(first_got if stage == 0 else second_got).at[group * 2 + part, off],
+            send_sem=rs_send.at[index], recv_sem=rs_recv.at[index],
             device_id=device_at(spot, axis, peer), device_id_type=MESH)
-
-    def own_rows(part):
-        return piece(part, 1, spot[PLANE[part][0]], spot[PLANE[part][1]])
 
     def rows_of(z):
         part = z // 4
@@ -288,28 +327,44 @@
             src_ref=where, dst_ref=where, send_sem=fw_send.at[part * 4 + off], recv_sem=fw_recv.at[part * 4 + off],
             device_id=sibling, device_id_type=MESH)
 
-    arrive(CHUNKS - 1)
-    for part in range(2):
-        strip_of(part)
-        pair_copy(part).start()
-    for part in range(2):
-        pair_copy(part).wait_recv()
-        for slot in range(part * 4, part * 4 + 4):
-            g[core, slot] += pair_got[slot]
-        for off in (2, 1, 3):
-            rs_copy(part, 0, off).start()
-    for part in range(2):
-        rows = piece(part, 0, spot[PLANE[part][0]], 0)
-        for off in (1, 3, 2):
-            rs_copy(part, 0, off).wait_recv()
-        g[core, pl.ds(part * 4, 4), :, rows, :] += first_got[part, 1] + first_got[part, 2] + first_got[part, 3]
-        for off in (2, 1, 3):
-            rs_copy(part, 1, off).start()
-    for part in range(2):
-        for off in (1, 3, 2):
-            rs_copy(part, 1, off).wait_recv()
-        g[core, pl.ds(part * 4, 4), :, own_rows(part), :] += (
-            second_got[part, 1] + second_got[part, 2] + second_got[part, 3])
+    def pair_send_out(group):
+        for part in range(2):
+            pair_copy(group, part).start()
+
+    def pair_add(group):
+        for part in range(2):
+            pair_copy(group, part).wait_recv()
+            for slot in range(part * 4 + group * 2, part * 4 + group * 2 + 2):
+                g[core, slot] += pair_got[slot]
+            for off in (2, 1, 3):
+                rs_copy(group, part, 0, off).start()
+
+    def plane_add(group, stage):
+        got_ref = first_got if stage == 0 else second_got
+        for part in range(2):
+            for off in (1, 3, 2):
+                rs_copy(group, part, stage, off).wait_recv()
+            rows = piece(part, stage, spot[PLANE[part][0]], spot[PLANE[part][1]])
+            which = group * 2 + part
+            g[core, slots_of(group, part), :, rows, :] += got_ref[which, 1] + got_ref[which, 2] + got_ref[which, 3]
+            if stage == 0:
+                for off in (2, 1, 3):
+                    rs_copy(group, part, 1, off).start()
+
+    lax.fori_loop(0, GATE + 1, early_chunk, 0)
+    send_group(1)
+    lax.fori_loop(GATE + 1, CHUNKS, early_chunk, 0)
+    pair_send_out(0)
+    late_chunk(0, 0)
+    pair_add(0)
+    lax.fori_loop(1, 4, late_chunk, 0)
+    plane_add(0, 0)
+    lax.fori_loop(4, CHUNKS, late_chunk, 0)
+    pair_send_out(1)
+    plane_add(0, 1)
+    pair_add(1)
+    plane_add(1, 0)
+    plane_add(1, 1)
     z_order = (4, 3, 5, 2, 6, 1, 7)
     for off in z_order:
         z_copy(off).start()
@@ -338,7 +393,8 @@
             ag_copy(part, 0, off).wait_recv()
             forward_copy(part, off).start()
     for off in range(1, GROUP):
-        start_copy(off).wait_recv()
+        for group in range(2):
+            start_copy(group, off).wait_recv()
     for part in range(2):
         for off in range(4):
             forward_copy(part, off).wait_recv()
@@ -348,7 +404,7 @@
 
     def full(kind):
         return jnp.concatenate(
-            [cat(*[o[(i + j) % 2, j // 2 * 4 + i, kind] for j in range(4)]) for i in range(4)], axis=0)
+            [cat(*[o[SLOT_OF[(i, j)] + (kind,)] for j in range(4)]) for i in range(4)], axis=0)
 
     def put(high_ref, low_ref, col, value):
         high, low = split(value)
@@ -397,10 +453,12 @@
         return carry
 
     lax.fori_loop(0, ITERS, step, 0)
-    weights_ref[...] = v_ref[aligned(me * OWN, OWN), :].T.reshape(2, BEAMS, OWN)
+    mine = jnp.concatenate([v_ref[virtual(0), :], v_ref[virtual(1), :]], axis=0)
+    weights_ref[...] = mine.T.reshape(2, BEAMS, OWN)
 
     vh, vl = split(v_ref[...].T)
     left = jnp.concatenate([vh, vl], axis=0)
+    tap_fetch.wait()
     taps = tap_ref[:, aligned(me * PART, PART)].astype(F32) / 2048.0
     beams = ([], [])
     for frame in range(FRAMES):
@@ -506,18 +564,21 @@
 
     for off in range(1, GROUP):
         last_copy(off).wait_send()
-        start_copy(off).wait_send()
-        for chunk in range(CHUNKS):
-            sample_copy(chunk, off).wait_send()
+        for group in range(2):
+            start_copy(group, off).wait_send()
+            for chunk in range(CHUNKS):
+                sample_copy(group, chunk, off).wait_send()
         for part in range(2):
             for stage in range(2):
-                rs_copy(part, stage, off).wait_send()
+                for group in range(2):
+                    rs_copy(group, part, stage, off).wait_send()
                 ag_copy(part, stage, off).wait_send()
     for off in range(1, 8):
         z_copy(off).wait_send()
         az_copy(off).wait_send()
     for part in range(2):
-        pair_copy(part).wait_send()
+        for group in range(2):
+            pair_copy(group, part).wait_send()
         for off in range(4):
             forward_copy(part, off).wait_send()
 
@@ -530,6 +591,11 @@
     def _():
         for off in order:
             cross_copy(off).wait_send()
+
+
+def finish_kernel(spectra_ref, weights_ref, spectra_out, weights_out):
+    spectra_out[...] = spectra_ref[...]
+    weights_out[...] = weights_ref[...]
 
 
 def body(samples, shift_bin, start_vectors, tap_table):
@@ -538,18 +604,20 @@
     hbm = pl.BlockSpec(memory_space=pl.ANY)
     dma = pltpu.SemaphoreType.DMA
     scratch = [
+        ((2, BEAMS, OWN), jnp.int32),
+        ((TAPS, CHANNELS), jnp.int32),
         ((CHUNKS, 2, ELEMS, CHUNK), F32),
         ((ELEMS, 2 * BEAMS), F32),
         ((2, 8, CHUNK), F32),
-        ((ELEMS, 2 * CHUNK), BF16),
-        ((ELEMS, 2 * CHUNK), BF16),
-        ((ELEMS, 2 * CHUNK), BF16),
-        ((ELEMS, 2 * CHUNK), BF16),
+        ((CHUNKS, ELEMS, 2 * CHUNK), BF16),
+        ((CHUNKS, ELEMS, 2 * CHUNK), BF16),
+        ((CHUNKS, ELEMS, 2 * CHUNK), BF16),
+        ((CHUNKS, ELEMS, 2 * CHUNK), BF16),
         ((2, 8, 3, BLOCK, BLOCK), F32),
         ((2, 8, 3, BLOCK, BLOCK), F32),
         ((8, 3, BLOCK, BLOCK), F32),
-        ((2, 4, 4, 3, 32, BLOCK), F32),
-        ((2, 4, 4, 3, 8, BLOCK), F32),
+        ((4, 4, 2, 3, 32, BLOCK), F32),
+        ((4, 4, 2, 3, 8, BLOCK), F32),
         ((8, 3, 8, BLOCK), F32),
         ((ELEMS, 2 * BEAMS), F32),
         ((ELEMS, 4 * ELEMS), BF16),
@@ -564,8 +632,8 @@
         ((GROUP, 2, FRAMES, QUARTER, PART), F32),
     ]
     semaphores = [
-        (CHUNKS, GROUP), (CHUNKS, GROUP), (CHUNKS,), (GROUP,), (GROUP,), None,
-        (2,), (2,), (16,), (16,), (8,), (8,), (8,), (8,), (16,), (16,),
+        (2 * CHUNKS, GROUP), (2 * CHUNKS, GROUP), (2 * CHUNKS,), (8,), (8,), None, (2,),
+        (4,), (4,), (32,), (32,), (8,), (8,), (8,), (8,), (16,), (16,),
         (8,), (8,), (GROUP,), (GROUP,), (GROUP,), (GROUP,), (GROUP,), (GROUP,),
     ]
     spectra, weights = pl.pallas_call(
@@ -574,7 +642,7 @@
             jax.ShapeDtypeStruct((2, FRAMES * QUARTER, CHANNELS), F32),
             jax.ShapeDtypeStruct((2, BEAMS, OWN), F32),
         ),
-        in_specs=[hbm, vmem, smem, vmem, hbm],
+        in_specs=[hbm, hbm, smem, hbm, hbm],
         out_specs=(vmem, vmem),
         scratch_shapes=[pltpu.VMEM(*entry) for entry in scratch]
         + [dma if shape is None else dma(shape) for shape in semaphores],
@@ -582,6 +650,16 @@
             collective_id=0, has_side_effects=True, vmem_limit_bytes=VMEM_LIMIT),
         name="beamformer",
     )(samples, start_vectors.transpose(0, 2, 1), shift_bin, tap_table, jnp.asarray(dft_tables()))
+    spectra, weights = pl.pallas_call(
+        finish_kernel,
+        out_shape=(
+            jax.ShapeDtypeStruct((2, FRAMES * QUARTER, CHANNELS), F32),
+            jax.ShapeDtypeStruct((2, BEAMS, OWN), F32),
+        ),
+        in_specs=[vmem, vmem],
+        out_specs=(vmem, vmem),
+        name="finish",
+    )(spectra, weights)
     spectra = spectra.reshape(2, FRAMES, QUARTER, CHANNELS).transpose(0, 2, 1, 3)
     return (spectra, weights.transpose(0, 2, 1))
 

time: 159 us -> 157 us (0.987)
  local copies, waits for them, and re-layouts: 3.24 us -> 0 us
    unnamed x2 -> x0, local copies, waits for them, and re-layouts: 3.24 us -> none
    pallas_call x0 -> x1, Pallas kernels: none -> 1.78 us  [body(): pl.pallas_call(finish_kernel, out_shape=(jax.ShapeDtypeStruct((2, FRAMES...]
where the time goes in v4:
time: 157 us
  Pallas kernels  156 us (99%)
    pallas_call x1, Pallas kernels, body(): pl.pallas_call(kernel, out_shape=(jax.ShapeDtypeStruct((2, FRAMES * QUART...  154 us

profile of v4, /device:TPU:40, one launch (start us, length us, event | category | flops | bytes accessed | tf_op | source)
XLA Modules:
  0.0 157.2 jit_solution(9612940548907762071)
XLA Ops:
  1.3 154.1 %beamformer.1 = (f32[2,48,1024]{2,1,0:T(8,128)}, f32[2,64,128]{2,1,0:T(8,128)}) custom-call(f32[2,128,3072]{2,1,0:T(8,128)} %x_ref.1, s32[2,64,128]{2,1,0:T(8,128)} %bitcast.5, s32[1]{0:T(128)S(6)} %copy.7.shift_ref, s32[4,1024]{1,0:T(4,128)} %tap_hbm.1, bf16[4,1024,1024]{2,1,0:T(8,128)(2,1)} %constant.2.clone.table_ref), custom_call_target="tpu_custom_call" | custom-call | tf_op jit(solution)/shard_map/beamformer/pallas_call | solution.py:639
  155.4 1.8 %finish.1 = (f32[2,48,1024]{2,1,0:T(8,128)}, f32[2,64,128]{2,1,0:T(8,128)}) custom-call(f32[2,48,1024]{2,1,0:T(8,128)} %get-tuple-element.6.spectra_ref, f32[2,64,128]{2,1,0:T(8,128)} %get-tuple-element.7.weights_ref), custom_call_target="tpu_custom_call" | custom-call | tf_op jit(solution)/shard_map/finish/pallas_call | solution.py:653

commit v5 on v4

--- a/solution.py
+++ b/solution.py
@@ -310,21 +310,22 @@
             src_ref=where, dst_ref=where, send_sem=az_send.at[off], recv_sem=az_recv.at[off],
             device_id=device_at(spot, "z", lax.rem(mine + off, 8)), device_id_type=MESH)
 
-    def ag_copy(part, stage, off):
+    def ag_copy(group, part, stage, off):
         axis = PLANE[part][stage]
         peer = lax.rem(spot[axis] + off, 4)
         rows = piece(part, stage, spot[PLANE[part][0]], spot[PLANE[part][1]])
-        where = o.at[core, pl.ds(part * 4, 4), :, rows, :]
-        return pltpu.make_async_remote_copy(
-            src_ref=where, dst_ref=where,
-            send_sem=ag_send.at[part * 8 + stage * 4 + off], recv_sem=ag_recv.at[part * 8 + stage * 4 + off],
+        where = o.at[core, slots_of(group, part), :, rows, :]
+        index = group * 16 + part * 8 + stage * 4 + off
+        return pltpu.make_async_remote_copy(
+            src_ref=where, dst_ref=where, send_sem=ag_send.at[index], recv_sem=ag_recv.at[index],
             device_id=device_at(spot, axis, peer), device_id_type=MESH)
 
-    def forward_copy(part, off):
+    def forward_copy(group, part, off):
         origin = lax.rem(spot[PLANE[part][0]] + 4 - off, 4)
-        where = o.at[core, pl.ds(part * 4, 4), :, aligned(origin * 32, 32), :]
-        return pltpu.make_async_remote_copy(
-            src_ref=where, dst_ref=where, send_sem=fw_send.at[part * 4 + off], recv_sem=fw_recv.at[part * 4 + off],
+        where = o.at[core, slots_of(group, part), :, aligned(origin * 32, 32), :]
+        index = group * 8 + part * 4 + off
+        return pltpu.make_async_remote_copy(
+            src_ref=where, dst_ref=where, send_sem=fw_send.at[index], recv_sem=fw_recv.at[index],
             device_id=sibling, device_id_type=MESH)
 
     def pair_send_out(group):
@@ -351,6 +352,91 @@
                 for off in (2, 1, 3):
                     rs_copy(group, part, 1, off).start()
 
+    z_order = (4, 3, 5, 2, 6, 1, 7)
+    mine = spot["z"]
+
+    def group_of(z):
+        return lax.rem(z // 2, 2)
+
+    def z_start(group):
+        for off in z_order:
+            @pl.when(group_of(lax.rem(mine + off, 8)) == group)
+            def _():
+                z_copy(off).start()
+
+    def z_sum(group):
+        @pl.when(group_of(mine) == group)
+        def _():
+            for off in range(1, 8):
+                z_copy(off).wait_recv()
+            total = g[core, mine, :, rows_of(mine), :]
+            for off in range(1, 8):
+                total = total + z_got[off]
+            o[core, mine, :, rows_of(mine), :] = total
+            for off in z_order:
+                az_copy(off).start()
+
+    def z_gather(group):
+        for off in range(1, 8):
+            @pl.when(group_of(lax.rem(mine + 8 - off, 8)) == group)
+            def _():
+                az_copy(off).wait_recv()
+        for part in range(2):
+            for off in (2, 1, 3):
+                ag_copy(group, part, 1, off).start()
+
+    def ag_middle(group):
+        for part in range(2):
+            for off in (1, 3, 2):
+                ag_copy(group, part, 1, off).wait_recv()
+            for off in (2, 1, 3):
+                ag_copy(group, part, 0, off).start()
+            forward_copy(group, part, 0).start()
+
+    def ag_last(group):
+        for off in (1, 3, 2):
+            for part in range(2):
+                ag_copy(group, part, 0, off).wait_recv()
+                forward_copy(group, part, off).start()
+
+    def ag_done(group):
+        for part in range(2):
+            for off in range(4):
+                forward_copy(group, part, off).wait_recv()
+
+    plain_scale = 1.0 / SAMPLES
+    cyc_scale = 1.0 / math.sqrt(SAMPLES * ELEMS)
+
+    def put(high_ref, low_ref, row, kind, col, value):
+        rows = pl.ds(row * BLOCK, BLOCK)
+        cols = pl.ds(kind * ELEMS + col * BLOCK, BLOCK)
+        high_ref[rows, cols], low_ref[rows, cols] = split(value)
+
+    def prepare(group):
+        for parity in range(2):
+            for slot in range(8):
+                if slot // 2 % 2 != group:
+                    continue
+                i, j = SLOTS[parity][slot]
+                for imag in (0, 1):
+                    block = o[parity, slot, 1 + imag] * cyc_scale
+                    put(ah, al, i, imag, j, block)
+                    put(bh, bl, j, imag, i, -block.T if imag else block.T)
+                block = o[parity, slot, 0] * plain_scale
+                turned_block = block.T
+                if i < j:
+                    put(ah, al, i, 2, j, block)
+                    put(ah, al, j, 2, i, turned_block)
+                elif i > j:
+                    put(ah, al, i, 3, j, block)
+                    put(ah, al, j, 3, i, -turned_block)
+                else:
+                    row_ids = lax.broadcasted_iota(jnp.int32, (BLOCK, BLOCK), 0)
+                    col_ids = lax.broadcasted_iota(jnp.int32, (BLOCK, BLOCK), 1)
+                    put(ah, al, i, 2, i, jnp.where(row_ids <= col_ids, block, turned_block))
+                    put(ah, al, i, 3, i, jnp.where(
+                        row_ids > col_ids, block, jnp.where(row_ids < col_ids, -turned_block, 0.0)))
+
     lax.fori_loop(0, GATE + 1, early_chunk, 0)
     send_group(1)
     lax.fori_loop(GATE + 1, CHUNKS, early_chunk, 0)
@@ -362,67 +448,26 @@
     lax.fori_loop(4, CHUNKS, late_chunk, 0)
     pair_send_out(1)
     plane_add(0, 1)
+    z_start(0)
     pair_add(1)
+    z_sum(0)
     plane_add(1, 0)
     plane_add(1, 1)
-    z_order = (4, 3, 5, 2, 6, 1, 7)
-    for off in z_order:
-        z_copy(off).start()
-    mine = spot["z"]
-    total = g[core, mine, :, rows_of(mine), :]
-    for off in range(1, 8):
-        z_copy(off).wait_recv()
-    for off in range(1, 8):
-        total = total + z_got[off]
-    o[core, mine, :, rows_of(mine), :] = total
-    for off in z_order:
-        az_copy(off).start()
-    for off in range(1, 8):
-        az_copy(off).wait_recv()
-    for part in range(2):
-        for off in (2, 1, 3):
-            ag_copy(part, 1, off).start()
-    for part in range(2):
-        for off in (1, 3, 2):
-            ag_copy(part, 1, off).wait_recv()
-        for off in (2, 1, 3):
-            ag_copy(part, 0, off).start()
-        forward_copy(part, 0).start()
-    for off in (1, 3, 2):
-        for part in range(2):
-            ag_copy(part, 0, off).wait_recv()
-            forward_copy(part, off).start()
+    z_start(1)
+    z_gather(0)
+    ag_middle(0)
+    z_sum(1)
+    ag_last(0)
+    z_gather(1)
+    ag_done(0)
+    prepare(0)
+    ag_middle(1)
     for off in range(1, GROUP):
         for group in range(2):
             start_copy(group, off).wait_recv()
-    for part in range(2):
-        for off in range(4):
-            forward_copy(part, off).wait_recv()
-
-    plain_scale = 1.0 / SAMPLES
-    cyc_scale = 1.0 / math.sqrt(SAMPLES * ELEMS)
-
-    def full(kind):
-        return jnp.concatenate(
-            [cat(*[o[SLOT_OF[(i, j)] + (kind,)] for j in range(4)]) for i in range(4)], axis=0)
-
-    def put(high_ref, low_ref, col, value):
-        high, low = split(value)
-        high_ref[:, col * ELEMS:(col + 1) * ELEMS] = high
-        low_ref[:, col * ELEMS:(col + 1) * ELEMS] = low
-
-    packed = full(0) * plain_scale
-    flipped = packed.T
-    row_ids = lax.broadcasted_iota(jnp.int32, (ELEMS, ELEMS), 0)
-    col_ids = lax.broadcasted_iota(jnp.int32, (ELEMS, ELEMS), 1)
-    put(ah, al, 2, jnp.where(row_ids <= col_ids, packed, flipped))
-    put(ah, al, 3, jnp.where(row_ids > col_ids, packed, jnp.where(row_ids < col_ids, -flipped, 0.0)))
-    cyc_real = full(1) * cyc_scale
-    put(ah, al, 0, cyc_real)
-    put(bh, bl, 0, cyc_real.T)
-    cyc_imag = full(2) * cyc_scale
-    put(ah, al, 1, cyc_imag)
-    put(bh, bl, 1, -cyc_imag.T)
+    ag_last(1)
+    ag_done(1)
+    prepare(1)
 
     lane = lax.broadcasted_iota(jnp.int32, (ELEMS, 2 * BEAMS), 1)
 
@@ -462,12 +507,13 @@
     taps = tap_ref[:, aligned(me * PART, PART)].astype(F32) / 2048.0
     beams = ([], [])
     for frame in range(FRAMES):
-        pieces = [xg[frame * 2 + half, kind] for kind in range(2) for half in range(2)]
-        xh, xl = split(cat(*pieces))
+        xh = cat(rh[frame * 2], rh[frame * 2 + 1])
+        xl = cat(rl[frame * 2], rl[frame * 2 + 1])
         both = dot_nn(left, xh)
         out = both[:2 * BEAMS] + both[2 * BEAMS:] + dot_nn(vh, xl)
-        beams[0].append(out[:BEAMS, :PART] + out[BEAMS:, PART:])
-        beams[1].append(out[:BEAMS, PART:] - out[BEAMS:, :PART])
+        top, low = out[:BEAMS], out[BEAMS:]
+        beams[0].append(cat(*[top[:, c:c + CHUNK] + low[:, c + CHUNK:c + 2 * CHUNK] for c in (0, 2 * CHUNK)]))
+        beams[1].append(cat(*[top[:, c + CHUNK:c + 2 * CHUNK] - low[:, c:c + CHUNK] for c in (0, 2 * CHUNK)]))
 
     def filtered(kind, frame):
         total = None
@@ -572,7 +618,7 @@
             for stage in range(2):
                 for group in range(2):
                     rs_copy(group, part, stage, off).wait_send()
-                ag_copy(part, stage, off).wait_send()
+                    ag_copy(group, part, stage, off).wait_send()
     for off in range(1, 8):
         z_copy(off).wait_send()
         az_copy(off).wait_send()
@@ -580,7 +626,8 @@
         for group in range(2):
             pair_copy(group, part).wait_send()
         for off in range(4):
-            forward_copy(part, off).wait_send()
+            for group in range(2):
+                forward_copy(group, part, off).wait_send()
 
     @pl.when(near_out)
     def _():
@@ -633,8 +680,8 @@
     ]
     semaphores = [
         (2 * CHUNKS, GROUP), (2 * CHUNKS, GROUP), (2 * CHUNKS,), (8,), (8,), None, (2,),
-        (4,), (4,), (32,), (32,), (8,), (8,), (8,), (8,), (16,), (16,),
-        (8,), (8,), (GROUP,), (GROUP,), (GROUP,), (GROUP,), (GROUP,), (GROUP,),
+        (4,), (4,), (32,), (32,), (8,), (8,), (8,), (8,), (32,), (32,),
+        (16,), (16,), (GROUP,), (GROUP,), (GROUP,), (GROUP,), (GROUP,), (GROUP,),
     ]
     spectra, weights = pl.pallas_call(
         kernel,

time: 157 us -> 150 us (0.955)
  Pallas kernels: 156 us -> 148 us
    pallas_call x1, Pallas kernels: 154 us -> 146 us  [body(): pl.pallas_call(kernel, out_shape=(jax.ShapeDtypeStruct((2, FRAMES * QUART...]
where the time goes in v5:
time: 150 us; the launch traced here: 149 us
  Pallas kernels  148 us (99%)
    pallas_call x1, Pallas kernels, body(): pl.pallas_call(kernel, out_shape=(jax.ShapeDtypeStruct((2, FRAMES * QUART...  146 us

profile of v5, /device:TPU:40, one launch (start us, length us, event | category | flops | bytes accessed | tf_op | source)
XLA Modules:
  0.0 149.4 jit_solution(11897045650541856991)
XLA Ops:
  1.3 146.4 %beamformer.1 = (f32[2,48,1024]{2,1,0:T(8,128)}, f32[2,64,128]{2,1,0:T(8,128)}) custom-call(f32[2,128,3072]{2,1,0:T(8,128)} %x_ref.1, s32[2,64,128]{2,1,0:T(8,128)} %bitcast.5, s32[1]{0:T(128)S(6)} %copy.7.shift_ref, s32[4,1024]{1,0:T(4,128)} %tap_hbm.1, bf16[4,1024,1024]{2,1,0:T(8,128)(2,1)} %constant.2.clone.table_ref), custom_call_target="tpu_custom_call" | custom-call | tf_op jit(solution)/shard_map/beamformer/pallas_call | solution.py:686
  147.7 1.8 %finish.1 = (f32[2,48,1024]{2,1,0:T(8,128)}, f32[2,64,128]{2,1,0:T(8,128)}) custom-call(f32[2,48,1024]{2,1,0:T(8,128)} %get-tuple-element.6.spectra_ref, f32[2,64,128]{2,1,0:T(8,128)} %get-tuple-element.7.weights_ref), custom_call_target="tpu_custom_call" | custom-call | tf_op jit(solution)/shard_map/finish/pallas_call | solution.py:700

commit v6 on v5

--- a/solution.py
+++ b/solution.py
@@ -27,12 +27,11 @@
 F32 = jnp.float32
 BF16 = jnp.bfloat16
 MESH = pl.DeviceIdType.MESH
-VMEM_LIMIT = 56 * 1024 * 1024
+VMEM_LIMIT = 46 * 1024 * 1024
 
 CHUNK = 128
 EARLY = 96
 LATE = OWN - EARLY
-GATE = 4
 CHUNKS = SPAN // GROUP // CHUNK
 BLOCK = 128
 SIZES = {"core": 2, "x": 4, "y": 4, "z": 8}
@@ -182,13 +181,12 @@
             own_copy(group, chunk).start()
 
     send_group(0)
+    send_group(1)
     table_copy.start()
     start_fetch.wait()
     starts = (start_ref[...].reshape(2 * BEAMS, OWN).astype(F32) - 4.5).T
     for group in range(2):
         sg[virtual(group), :] = starts[firsts[group]:firsts[group] + counts[group]]
-        for off in range(1, GROUP):
-            start_copy(group, off).start()
 
     rows8 = lax.broadcasted_iota(jnp.int32, (8, CHUNK), 0)
     lanes = lax.broadcasted_iota(jnp.int32, (8, CHUNK), 1)
@@ -437,9 +435,7 @@
                     put(ah, al, i, 3, i, jnp.where(
                         row_ids > col_ids, block, jnp.where(row_ids < col_ids, -turned_block, 0.0)))
 
-    lax.fori_loop(0, GATE + 1, early_chunk, 0)
-    send_group(1)
-    lax.fori_loop(GATE + 1, CHUNKS, early_chunk, 0)
+    lax.fori_loop(0, CHUNKS, early_chunk, 0)
     pair_send_out(0)
     late_chunk(0, 0)
     pair_add(0)
@@ -449,6 +445,9 @@
     pair_send_out(1)
     plane_add(0, 1)
     z_start(0)
+    for group in range(2):
+        for off in range(1, GROUP):
+            start_copy(group, off).start()
     pair_add(1)
     z_sum(0)
     plane_add(1, 0)
@@ -460,8 +459,8 @@
     ag_last(0)
     z_gather(1)
     ag_done(0)
+    ag_middle(1)
     prepare(0)
-    ag_middle(1)
     for off in range(1, GROUP):
         for group in range(2):
             start_copy(group, off).wait_recv()
@@ -705,6 +704,7 @@
         ),
         in_specs=[vmem, vmem],
         out_specs=(vmem, vmem),
+        compiler_params=pltpu.CompilerParams(vmem_limit_bytes=4 * 1024 * 1024),
         name="finish",
     )(spectra, weights)
     spectra = spectra.reshape(2, FRAMES, QUARTER, CHANNELS).transpose(0, 2, 1, 3)

time: 150 us -> 148 us (0.987)
  Pallas kernels: 148 us -> 142 us
  local copies, waits for them, and re-layouts: 0 us -> 3.44 us
    pallas_call x1, Pallas kernels: 146 us -> 141 us  [body(): pl.pallas_call(kernel, out_shape=(jax.ShapeDtypeStruct((2, FRAMES * QUART...]
    unnamed x0 -> x6, local copies, waits for them, and re-layouts: none -> 3.44 us
where the time goes in v6:
time: 148 us; the launch traced here: 147 us
  Pallas kernels  142 us (96%)
  local copies, waits for them, and re-layouts  3.44 us (2%)
    pallas_call x1, Pallas kernels, body(): pl.pallas_call(kernel, out_shape=(jax.ShapeDtypeStruct((2, FRAMES * QUART...  141 us
    unnamed x6, local copies, waits for them, and re-layouts  3.44 us

profile of v6, /device:TPU:40, one launch (start us, length us, event | category | flops | bytes accessed | tf_op | source)
XLA Modules:
  0.0 146.7 jit_solution(7440966832338180199)
XLA Ops:
  1.3 0.0 copy-start
  1.3 1.9 %copy-done = f32[2,128,3072]{2,1,0:T(8,128)S(1)} copy-done((f32[2,128,3072]{2,1,0:T(8,128)S(1)}, f32[2,128,3072]{2,1,0:T(8,128)}, u32[]{:S(2)}) %copy-start) | copy-done | bytes 3145752
  3.2 0.0 copy-start.1
  3.2 0.8 copy-done.1
  4.0 0.0 copy-start.2
  4.0 0.7 copy-done.2
  4.7 141.2 %beamformer.1 = (f32[2,48,1024]{2,1,0:T(8,128)S(1)}, f32[2,64,128]{2,1,0:T(8,128)S(1)}) custom-call(f32[2,128,3072]{2,1,0:T(8,128)S(1)} %copy-done, s32[2,64,128]{2,1,0:T(8,128)S(1)} %bitcast.5, s32[1]{0:T(128)S(6)} %copy.7.shift_ref, s32[4,1024]{1,0:T(4,128)S(1)} %copy-done.2, bf16[4,1024,1024]{2,1,0:T(8,128)(2,1)} %constant.2.clone.table_ref), custom_call_target="tpu_custom_call" | custom-call | tf_op jit(solution)/shard_map/beamformer/pallas_call | solution.py:685
  145.9 0.8 finish.1
Async XLA Ops:
  1.3 1.9 %copy-start = (f32[2,128,3072]{2,1,0:T(8,128)S(1)}, f32[2,128,3072]{2,1,0:T(8,128)}, u32[]{:S(2)}) copy-start(f32[2,128,3072]{2,1,0:T(8,128)} %x_ref.1) | copy-start | bytes 9437188
  3.2 0.8 copy-start.1
  4.0 0.7 copy-start.2

commit v7 on v6

--- a/solution.py
+++ b/solution.py
@@ -695,7 +695,8 @@
         compiler_params=pltpu.CompilerParams(
             collective_id=0, has_side_effects=True, vmem_limit_bytes=VMEM_LIMIT),
         name="beamformer",
-    )(samples, start_vectors.transpose(0, 2, 1), shift_bin, tap_table, jnp.asarray(dft_tables()))
+    )(*[pltpu.with_memory_space_constraint(value, pltpu.HBM) for value in (samples, start_vectors.transpose(0, 2, 1))],
+      shift_bin, pltpu.with_memory_space_constraint(tap_table, pltpu.HBM), jnp.asarray(dft_tables()))
     spectra, weights = pl.pallas_call(
         finish_kernel,
         out_shape=(

time: 148 us -> 145 us (0.980)
  local copies, waits for them, and re-layouts: 3.44 us -> 0 us
    unnamed x6 -> x0, local copies, waits for them, and re-layouts: 3.44 us -> none
where the time goes in v7:
time: 145 us; the launch traced here: 144 us
  Pallas kernels  143 us (99%)
    pallas_call x1, Pallas kernels, body(): pl.pallas_call(kernel, out_shape=(jax.ShapeDtypeStruct((2, FRAMES * QUART...  142 us

profile of v7, /device:TPU:40, one launch (start us, length us, event | category | flops | bytes accessed | tf_op | source)
XLA Modules:
  0.0 144.2 jit_solution(15958050543727162375)
XLA Ops:
  1.3 142.1 %beamformer.1 = (f32[2,48,1024]{2,1,0:T(8,128)S(1)}, f32[2,64,128]{2,1,0:T(8,128)S(1)}) custom-call(f32[2,128,3072]{2,1,0:T(8,128)} %x_ref.1, s32[2,64,128]{2,1,0:T(8,128)} %bitcast.5, s32[1]{0:T(128)S(6)} %copy.7.shift_ref, s32[4,1024]{1,0:T(4,128)} %tap_hbm.1, bf16[4,1024,1024]{2,1,0:T(8,128)(2,1)} %constant.2.clone.table_ref), custom_call_target="tpu_custom_call" | custom-call | tf_op jit(solution)/shard_map/beamformer/pallas_call | solution.py:685
  143.4 0.8 finish.1

commit v8 on v7

--- a/solution.py
+++ b/solution.py
@@ -38,7 +38,7 @@
 PLANE = (("x", "y"), ("y", "x"))
 SLOTS = (
     ((0, 0), (0, 2), (1, 1), (1, 3), (2, 0), (2, 2), (3, 1), (3, 3)),
-    ((0, 1), (1, 0), (0, 3), (3, 0), (1, 2), (2, 1), (2, 3), (3, 2)),
+    ((0, 1), (1, 0), (0, 3), (2, 3), (1, 2), (2, 1), (3, 0), (3, 2)),
 )
 SLOT_OF = {block: (parity, slot) for parity in range(2) for slot, block in enumerate(SLOTS[parity])}
 
@@ -240,26 +240,36 @@
 
     def early_chunk(chunk, carry):
         arrive(0, chunk)
-        right = right_of(chunk, front)
-        for imag in (0, 1):
-            add_blocks(1 + imag, 0, 0, dot_nt(left_of(uh, ul, chunk, front, imag), right))
-        add_blocks(0, 0, 0, jnp.where(
-            triangle(3 * BLOCK), dot_nt(left_of(rh, rl, chunk, front, 0), right),
-            dot_nt(left_of(rh, rl, chunk, front, 1), right)))
+        out = dot_nt(jnp.concatenate(
+            [left_of(uh, ul, chunk, front, 0), left_of(uh, ul, chunk, front, 1),
+             left_of(rh, rl, chunk, front, 0), left_of(rh, rl, chunk, front, 1)], axis=0), right_of(chunk, front))
+        size = 3 * BLOCK
+        add_blocks(1, 0, 0, out[:size])
+        add_blocks(2, 0, 0, out[size:2 * size])
+        add_blocks(0, 0, 0, jnp.where(triangle(size), out[2 * size:3 * size], out[3 * size:]))
         return carry
+
+    def late_columns(chunk):
+        last = right_of(chunk, back)
+        out = dot_nt(jnp.concatenate(
+            [left_of(rh, rl, chunk, front, 0), left_of(uh, ul, chunk, front, 0), left_of(uh, ul, chunk, front, 1),
+             left_of(rh, rl, chunk, back, 0)], axis=0), last)
+        for kind in range(3):
+            add_blocks(kind, 0, 3, out[kind * 3 * BLOCK:(kind + 1) * 3 * BLOCK])
+        return out[9 * BLOCK:]
+
+    def late_rows(chunk, corner):
+        out = dot_nt(jnp.concatenate(
+            [left_of(rh, rl, chunk, back, 1), left_of(uh, ul, chunk, back, 0), left_of(uh, ul, chunk, back, 1)],
+            axis=0), right_of(chunk, pl.ds(0, ELEMS)))
+        add_blocks(0, 3, 0, out[:BLOCK, :3 * BLOCK])
+        add_blocks(0, 3, 3, jnp.where(triangle(BLOCK), corner, out[:BLOCK, 3 * BLOCK:]))
+        for kind in (1, 2):
+            add_blocks(kind, 3, 0, out[kind * BLOCK:(kind + 1) * BLOCK])
 
     def late_chunk(chunk, carry):
         arrive(1, chunk)
-        right = right_of(chunk, pl.ds(0, ELEMS))
-        last = right_of(chunk, back)
-        for imag in (0, 1):
-            add_blocks(1 + imag, 3, 0, dot_nt(left_of(uh, ul, chunk, back, imag), right))
-            add_blocks(1 + imag, 0, 3, dot_nt(left_of(uh, ul, chunk, front, imag), last))
-        add_blocks(0, 0, 3, dot_nt(left_of(rh, rl, chunk, front, 0), last))
-        low = dot_nt(left_of(rh, rl, chunk, back, 1), right)
-        add_blocks(0, 3, 0, low[:, :3 * BLOCK])
-        add_blocks(0, 3, 3, jnp.where(
-            triangle(BLOCK), dot_nt(left_of(rh, rl, chunk, back, 0), last), low[:, 3 * BLOCK:]))
+        late_rows(chunk, late_columns(chunk))
         return carry
 
     sibling = device_at(spot, "core", 1 - core)
@@ -441,14 +451,18 @@
     pair_add(0)
     lax.fori_loop(1, 4, late_chunk, 0)
     plane_add(0, 0)
-    lax.fori_loop(4, CHUNKS, late_chunk, 0)
-    pair_send_out(1)
+    lax.fori_loop(4, CHUNKS - 1, late_chunk, 0)
+    arrive(1, CHUNKS - 1)
+    corner = late_columns(CHUNKS - 1)
+    pair_copy(1, 0).start()
+    late_rows(CHUNKS - 1, corner)
+    pair_copy(1, 1).start()
+    pair_add(1)
     plane_add(0, 1)
     z_start(0)
     for group in range(2):
         for off in range(1, GROUP):
             start_copy(group, off).start()
-    pair_add(1)
     z_sum(0)
     plane_add(1, 0)
     plane_add(1, 1)

time: 145 us -> 144 us (level)
  no operation moved by 1% of the time
where the time goes in v8:
time: 144 us
  Pallas kernels  143 us (99%)
    pallas_call x1, Pallas kernels, body(): pl.pallas_call(kernel, out_shape=(jax.ShapeDtypeStruct((2, FRAMES * QUART...  142 us

profile of v8, /device:TPU:40, one launch (start us, length us, event | category | flops | bytes accessed | tf_op | source)
XLA Modules:
  0.0 143.9 jit_solution(13909486339691616006)
XLA Ops:
  1.3 141.9 %beamformer.1 = (f32[2,48,1024]{2,1,0:T(8,128)S(1)}, f32[2,64,128]{2,1,0:T(8,128)S(1)}) custom-call(f32[2,128,3072]{2,1,0:T(8,128)} %x_ref.1, s32[2,64,128]{2,1,0:T(8,128)} %bitcast.5, s32[1]{0:T(128)S(6)} %copy.7.shift_ref, s32[4,1024]{1,0:T(4,128)} %tap_hbm.1, bf16[4,1024,1024]{2,1,0:T(8,128)(2,1)} %constant.2.clone.table_ref), custom_call_target="tpu_custom_call" | custom-call | tf_op jit(solution)/shard_map/beamformer/pallas_call | solution.py:699
  143.2 0.8 finish.1

commit v9 on v8

--- a/solution.py
+++ b/solution.py
@@ -519,11 +519,10 @@
     tap_fetch.wait()
     taps = tap_ref[:, aligned(me * PART, PART)].astype(F32) / 2048.0
     beams = ([], [])
+    both = dot_nn(left, cat(*[rh[chunk] for chunk in range(CHUNKS)]))
+    every = both[:2 * BEAMS] + both[2 * BEAMS:] + dot_nn(vh, cat(*[rl[chunk] for chunk in range(CHUNKS)]))
     for frame in range(FRAMES):
-        xh = cat(rh[frame * 2], rh[frame * 2 + 1])
-        xl = cat(rl[frame * 2], rl[frame * 2 + 1])
-        both = dot_nn(left, xh)
-        out = both[:2 * BEAMS] + both[2 * BEAMS:] + dot_nn(vh, xl)
+        out = every[:, frame * 4 * CHUNK:(frame + 1) * 4 * CHUNK]
         top, low = out[:BEAMS], out[BEAMS:]
         beams[0].append(cat(*[top[:, c:c + CHUNK] + low[:, c + CHUNK:c + 2 * CHUNK] for c in (0, 2 * CHUNK)]))
         beams[1].append(cat(*[top[:, c + CHUNK:c + 2 * CHUNK] - low[:, c:c + CHUNK] for c in (0, 2 * CHUNK)]))

time: 144 us -> 144 us (level)
  no operation moved by 1% of the time
where the time goes in v9:
time: 144 us
  Pallas kernels  143 us (99%)
    pallas_call x1, Pallas kernels, body(): pl.pallas_call(kernel, out_shape=(jax.ShapeDtypeStruct((2, FRAMES * QUART...  142 us

profile of v9, /device:TPU:40, one launch (start us, length us, event | category | flops | bytes accessed | tf_op | source)
XLA Modules:
  0.0 143.9 jit_solution(10926393510005916346)
XLA Ops:
  1.3 141.9 %beamformer.1 = (f32[2,48,1024]{2,1,0:T(8,128)S(1)}, f32[2,64,128]{2,1,0:T(8,128)S(1)}) custom-call(f32[2,128,3072]{2,1,0:T(8,128)} %x_ref.1, s32[2,64,128]{2,1,0:T(8,128)} %bitcast.5, s32[1]{0:T(128)S(6)} %copy.7.shift_ref, s32[4,1024]{1,0:T(4,128)} %tap_hbm.1, bf16[4,1024,1024]{2,1,0:T(8,128)(2,1)} %constant.2.clone.table_ref), custom_call_target="tpu_custom_call" | custom-call | tf_op jit(solution)/shard_map/beamformer/pallas_call | solution.py:698
  143.2 0.8 finish.1
